TPU v7x, 512 devices: a whole 4x8x8 slice. The times are simulated.
512 devices in a mesh: freq: 16 (over x, y_hi, core), tm: 32 (over y_lo, z).
Axes of the slice: x: 4, y: 8 (y_hi: 2, y_lo: 4; y = y_hi * 4 + y_lo), z: 8, core: 2. Of those that a mesh axis runs over, the one named last changes fastest.
Arguments:
- visibilities: float32 [32, 8, 4096], P('freq', None, 'tm'), may hold values from -6 to 6
- coherencies: bfloat16 [32, 8, 8, 4096], P('freq', None, None, 'tm'), may hold values from -2.09375 to 2.09375
- pairs: int32 [2, 4096], P(None, 'tm'), may hold values from 0 to 511, as said below
- gains_start: float32 [32, 8, 8, 512], P('freq'), may hold values from -0.9 to 1.9
- duals_start: float32 [32, 8, 8, 512], P('freq'), may hold values from -12 to 12
- poly_start: float32 [4, 8, 8, 512], replicated, may hold values from -0.6 to 1.6
Outputs:
- gains: float32 [32, 8, 8, 512], P('freq')
- duals: float32 [32, 8, 8, 512], P('freq')
- polynomial: float32 [4, 8, 8, 512], replicated
Inputs may be any that keep to these rules, and one draw needn't show every extreme that they name: `pairs`: each row names two different stations.
All inputs are finite; a program needn't handle non-finite values.
Results may differ from a plain program's by a relative error of at most 0.0003.
Values sent between devices are 32-bit elements; how exact they have to be, the bound alone decides.
No kernel may reach another device: no remote copies, remote signals or barrier semaphores. Data moves between devices by JAX's collectives and lax.ppermute only.
A program may use at most 64 MiB of HBM per device.

v0:
```python
import functools

import jax
import jax.numpy as jnp
import numpy as np
from jax import lax
from jax.experimental import pallas as pl
from jax.experimental.pallas import tpu as pltpu
from jax.sharding import PartitionSpec as P

ITERS = 2
RHO = 16.0
CHANS = 2
DIRS = 8
STATIONS = 512
ROWS = 128
POLY = 4
LANES = 128
CUTS = STATIONS // LANES
F32 = jnp.float32
BF16 = jnp.bfloat16


def adjoint(matrix):
    re, im = matrix
    return ([re[0], re[2], re[1], re[3]], [-im[0], -im[2], -im[1], -im[3]])


def product(left, right):
    lr, li = left
    rr, ri = right
    out_re, out_im = [], []
    for row in range(2):
        for col in range(2):
            a = 2 * row
            out_re.append(lr[a] * rr[col] - li[a] * ri[col] + lr[a + 1] * rr[col + 2] - li[a + 1] * ri[col + 2])
            out_im.append(lr[a] * ri[col] + li[a] * rr[col] + lr[a + 1] * ri[col + 2] + li[a + 1] * rr[col + 2])
    return (out_re, out_im)


def normal(matrix):
    re, im = matrix
    return [
        re[0] ** 2 + im[0] ** 2 + re[1] ** 2 + im[1] ** 2,
        re[2] ** 2 + im[2] ** 2 + re[3] ** 2 + im[3] ** 2,
        re[0] * re[2] + im[0] * im[2] + re[1] * re[3] + im[1] * im[3],
        im[0] * re[2] - re[0] * im[2] + im[1] * re[3] - re[1] * im[3],
    ]


def two_parts(x):
    high = x.astype(BF16)
    low = (x - high.astype(F32)).astype(BF16)
    return jnp.concatenate([high, low], axis=0)


def one_hot(pairs_ref):
    station = lax.broadcasted_iota(jnp.int32, (STATIONS, ROWS), 0)
    marks = [jnp.where(station == pairs_ref[i : i + 1, :], 1.0, 0.0) for i in range(2)]
    return jnp.concatenate(marks, axis=1).astype(BF16)


def sums_kernel(gathered, gains_ref, coh_ref, vis_ref, pairs_ref, out_ref, at_p, at_q, terms_p, terms_q, summed):
    hot = one_hot(pairs_ref)
    if gathered:
        rows = jnp.concatenate(
            [
                jnp.concatenate([gains_ref[k * CUTS + q] for q in range(CUTS)], axis=1)
                for k in range(DIRS)
            ],
            axis=0,
        )
    else:
        rows = gains_ref[...].reshape(CHANS * 8 * DIRS, STATIONS)
    count = rows.shape[0]
    found = jnp.dot(two_parts(rows), hot, preferred_element_type=F32)
    found = found[:count] + found[count:]
    at_p[...] = found[:, :ROWS]
    at_q[...] = found[:, ROWS:]

    def picked(ref, c, i):
        if gathered:
            return ref[pl.ds(c * 8 + i, DIRS, stride=CHANS * 8), :]
        return ref[pl.ds((c * 8 + i) * DIRS, DIRS), :]

    for c in range(CHANS):
        first = ([picked(at_p, c, i) for i in range(4)], [picked(at_p, c, i + 4) for i in range(4)])
        second = ([picked(at_q, c, i) for i in range(4)], [picked(at_q, c, i + 4) for i in range(4)])
        sky = [coh_ref[c, i].astype(F32) for i in range(8)]
        sky = (sky[:4], sky[4:])
        left = product(first, sky)
        right = product(sky, adjoint(second))
        model = product(left, adjoint(second))
        model = [jnp.sum(part, axis=0, keepdims=True) for part in model[0] + model[1]]
        rest = [
            jnp.broadcast_to(vis_ref[c, pl.ds(i, 1), :] - model[i], (DIRS, ROWS)) for i in range(8)
        ]
        rest = (rest[:4], rest[4:])
        grad_p = product(rest, adjoint(right))
        grad_q = product(adjoint(rest), left)
        for ref, terms in (
            (terms_p, grad_p[0] + grad_p[1] + normal(right)),
            (terms_q, grad_q[0] + grad_q[1] + normal(adjoint(left))),
        ):
            for i, term in enumerate(terms):
                ref[pl.ds((c * 12 + i) * DIRS, DIRS), :] = term
    terms = jnp.concatenate([terms_p[...], terms_q[...]], axis=1)
    count = terms.shape[0]
    total = lax.dot_general(
        two_parts(terms), hot, (((1,), (1,)), ((), ())), preferred_element_type=F32
    )
    total = total[:count] + total[count:]
    for q in range(CUTS):
        summed[q] = total[:, q * LANES : (q + 1) * LANES]
    for k in range(DIRS):
        for q in range(CUTS):
            out_ref[k * CUTS + q] = summed[q, pl.ds(k, CHANS * 12, stride=DIRS), :]


def share_sums(gains, coherencies, visibilities, pairs, gathered):
    rows = CHANS * 8 * DIRS
    terms = CHANS * 12 * DIRS
    return pl.pallas_call(
        functools.partial(sums_kernel, gathered),
        out_shape=jax.ShapeDtypeStruct((DIRS * CUTS, CHANS * 12, LANES), F32),
        scratch_shapes=[
            pltpu.VMEM((rows, ROWS), F32),
            pltpu.VMEM((rows, ROWS), F32),
            pltpu.VMEM((terms, ROWS), F32),
            pltpu.VMEM((terms, ROWS), F32),
            pltpu.VMEM((CUTS, terms, LANES), F32),
        ],
        name="sums",
    )(gains, coherencies, visibilities, pairs)


def basis_of(channel, count):
    x = (2.0 * channel.astype(F32) + 1.0) / count - 1.0
    return [1.0 + 0.0 * x, x, 1.5 * x * x - 0.5, 2.5 * x * x * x - 1.5 * x]


def inverse_gram(count):
    x = (2.0 * np.arange(count) + 1.0) / count - 1.0
    basis = np.stack([np.ones_like(x), x, 1.5 * x * x - 0.5, 2.5 * x**3 - 1.5 * x], axis=1)
    return np.linalg.inv(basis.T @ basis)


def weights_of(basis, gram):
    return [sum(float(gram[j, i]) * basis[i] for i in range(POLY)) for j in range(POLY)]


def own_kernel(count, index_ref, gains_ref, duals_ref, poly_ref, out_ref):
    freq, place = index_ref[0], index_ref[1]
    k = place // CUTS
    lanes = pl.ds(pl.multiple_of((place % CUTS) * LANES, LANES), LANES)
    chosen = lax.broadcasted_iota(jnp.int32, (DIRS, LANES), 0) == k

    def row(tile):
        return jnp.sum(jnp.where(chosen, tile, 0.0), axis=0, keepdims=True)

    for c in range(CHANS):
        basis = basis_of(freq * CHANS + c, count)
        for i in range(8):
            at = pl.ds(c * 8 + i, 1)
            out_ref[0, at, :] = row(gains_ref[c, i, :, lanes])
            out_ref[1, at, :] = row(duals_ref[c, i, :, lanes])
            prior = basis[0] * poly_ref[0, i, :, lanes]
            for j in range(1, POLY):
                prior += basis[j] * poly_ref[j, i, :, lanes]
            out_ref[2, at, :] = row(prior)


SMEM = pl.BlockSpec(memory_space=pltpu.SMEM)
VMEM = pl.BlockSpec(memory_space=pltpu.VMEM)


def own_share(index, gains, duals, poly, count):
    return pl.pallas_call(
        functools.partial(own_kernel, count),
        out_shape=jax.ShapeDtypeStruct((3, CHANS * 8, LANES), F32),
        in_specs=[SMEM, VMEM, VMEM, VMEM],
        name="own",
    )(index, gains, duals, poly)


def both(ref, i, step):
    return ref[pl.ds(i, CHANS, stride=step), :]


def updated(sums_ref, own_ref, gains_ref, damping, arrived, put):
    total = arrived[0]
    for n in range(1, arrived.shape[0]):
        total = total + arrived[n]
    sums_ref[...] = total
    gains = [both(gains_ref, i, 8) for i in range(8)]
    way = [
        both(sums_ref, i, 12) - both(own_ref.at[1], i, 8) - RHO * (gains[i] - both(own_ref.at[2], i, 8))
        for i in range(8)
    ]
    top, bottom, cross_re, cross_im = [both(sums_ref, i, 12) for i in range(8, 12)]
    shift = damping * 0.5 * (top + bottom) + RHO
    upper = top + shift
    lower = bottom + shift
    scale = 1.0 / (upper * lower - cross_re * cross_re - cross_im * cross_im)
    zeros = jnp.zeros_like(scale)
    inverse = (
        [lower * scale, -cross_re * scale, -cross_re * scale, upper * scale],
        [zeros, -cross_im * scale, cross_im * scale, zeros],
    )
    step = product((way[:4], way[4:]), inverse)
    step = step[0] + step[1]
    for i in range(8):
        put[pl.ds(i, CHANS, stride=8), :] = gains[i] + step[i]


def first_kernel(damping, arrived, own_ref, out_ref, sums_ref, new):
    updated(sums_ref, own_ref, own_ref.at[0], damping, arrived, new)
    value = new[...]
    for n in range(out_ref.shape[0]):
        out_ref[n] = value


def last_kernel(damping, count, gram, index_ref, arrived, own_ref, gains_ref, fit_ref, new, sums_ref):
    updated(sums_ref, own_ref, gains_ref, damping, arrived, new)
    mixed = new[...] + own_ref[1] / RHO
    weights = [weights_of(basis_of(index_ref[0] * CHANS + c, count), gram) for c in range(CHANS)]
    for core in range(2):
        parts = [
            sum(weights[c][2 * core + j] * mixed[c * 8 : (c + 1) * 8] for c in range(CHANS))
            for j in range(2)
        ]
        part = jnp.concatenate(parts, axis=0)
        for n in range(core, fit_ref.shape[0], 2):
            fit_ref[n] = part


def joined_kernel(arrived, gains_ref, out_ref):
    total = arrived[0]
    for n in range(1, arrived.shape[0]):
        total = total + arrived[n]
    gains = gains_ref[...]
    for n in range(out_ref.shape[0]):
        out_ref[n, pl.ds(0, 16), :] = gains
        out_ref[n, pl.ds(16, 16), :] = total


def end_kernel(count, index_ref, all_ref, other_ref, duals_ref, gains_out, duals_out, poly_out):
    freq = index_ref[0]
    core = freq % 2
    basis = [basis_of(freq * CHANS + c, count) for c in range(CHANS)]
    mine = [[jnp.where(core == 0, basis[c][j], basis[c][j + 2]) for j in range(2)] for c in range(CHANS)]
    his = [[jnp.where(core == 0, basis[c][j + 2], basis[c][j]) for j in range(2)] for c in range(CHANS)]
    every = CUTS * 32
    half = CUTS * 16
    for i in range(8):
        for q in range(CUTS):
            lanes = pl.ds(q * LANES, LANES)
            own = [all_ref[pl.ds(q * 32 + 16 + j * 8 + i, DIRS, stride=every), :] for j in range(2)]
            far = [other_ref[pl.ds(q * 16 + j * 8 + i, DIRS, stride=half), :] for j in range(2)]
            for j in range(2):
                poly_out[2 * core + j, i, :, lanes] = own[j]
                poly_out[2 - 2 * core + j, i, :, lanes] = far[j]
            for c in range(CHANS):
                gains = all_ref[pl.ds(q * 32 + c * 8 + i, DIRS, stride=every), :]
                gains_out[c, i, :, lanes] = gains
                prior = mine[c][0] * own[0] + mine[c][1] * own[1] + his[c][0] * far[0] + his[c][1] * far[1]
                duals_out[c, i, :, lanes] = duals_ref[c, i, :, lanes] + RHO * (gains - prior)


def exchanged(x, axis):
    return lax.all_to_all(x, axis, split_axis=0, concat_axis=0, tiled=True)


def shards(visibilities, coherencies, pairs, gains_start, duals_start, poly_start):
    freqs, times = lax.axis_size("freq"), lax.axis_size("tm")
    count = CHANS * freqs
    index = jnp.stack([lax.axis_index("freq"), lax.axis_index("tm")]).astype(jnp.int32)
    share = jax.ShapeDtypeStruct((CHANS * 8, LANES), F32)
    sums_scratch = pltpu.VMEM((CHANS * 12, LANES), F32)
    new_scratch = pltpu.VMEM((CHANS * 8, LANES), F32)

    own = own_share(index, gains_start, duals_start, poly_start, count)
    sums = exchanged(share_sums(gains_start, coherencies, visibilities, pairs, False), "tm")
    copies = pl.pallas_call(
        functools.partial(first_kernel, 12.0),
        out_shape=jax.ShapeDtypeStruct((times, CHANS * 8, LANES), F32),
        scratch_shapes=[sums_scratch, new_scratch],
        name="first",
    )(sums, own)
    gains = exchanged(copies, "tm")
    sums = exchanged(share_sums(gains, coherencies, visibilities, pairs, True), "tm")
    fits, mine = pl.pallas_call(
        functools.partial(last_kernel, 6.0, count, inverse_gram(count)),
        out_shape=(jax.ShapeDtypeStruct((freqs, 16, LANES), F32), share),
        in_specs=[SMEM, VMEM, VMEM, VMEM],
        scratch_shapes=[sums_scratch],
        name="last",
    )(index, sums, own, copies[0])
    fits = exchanged(fits, "freq")
    copies = pl.pallas_call(
        joined_kernel,
        out_shape=jax.ShapeDtypeStruct((times, 32, LANES), F32),
        name="joined",
    )(fits, mine)
    everything = exchanged(copies, "tm")
    other = lax.ppermute(everything[:, 16:], "freq", [(i, i ^ 1) for i in range(freqs)])
    block = (CHANS, 8, DIRS, STATIONS)
    return pl.pallas_call(
        functools.partial(end_kernel, count),
        out_shape=(
            jax.ShapeDtypeStruct(block, F32),
            jax.ShapeDtypeStruct(block, F32),
            jax.ShapeDtypeStruct((POLY, 8, DIRS, STATIONS), F32),
        ),
        in_specs=[SMEM, VMEM, VMEM, VMEM],
        name="end",
    )(index, everything.reshape(times * 32, LANES), other.reshape(times * 16, LANES), duals_start)


def solution(mesh):
    placed = (
        P("freq", None, "tm"),
        P("freq", None, None, "tm"),
        P(None, "tm"),
        P("freq", None, None, None),
        P("freq", None, None, None),
        P(),
    )
    return jax.shard_map(
        shards,
        mesh=mesh,
        in_specs=placed,
        out_specs=(P("freq", None, None, None), P("freq", None, None, None), P()),
        check_vma=False,
    )
```

profile of v0, /device:TPU:1, one launch (start us, length us, event | category | flops | bytes accessed | tf_op | source)
XLA Modules:
  0.0 124.3 jit_solution(5472052388025674764)
XLA Ops:
  0.6 2.3 %sums.2 = f32[32,24,128]{2,1,0:T(8,128)} custom-call(f32[2,8,8,512]{3,2,1,0:T(8,128)} %gains_ref.3, bf16[2,8,8,128]{3,2,1,0:T(8,128)(2,1)} %coh_ref.3, f32[2,8,128]{2,1,0:T(8,128)} %vis_ref.3, s32[2,128]{1,0:T(2,128)} %pairs_ref.3), custom_call_target="tpu_custom_call" | custom-call | tf_op jit(solution)/shard_map/sums/pallas_call | solution.py:123
  3.0 14.3 %all-to-all-start = ((f32[32,24,128]{2,1,0:T(8,128)}), f32[32,24,128]{2,1,0:T(8,128)S(1)}, u32[]{:S(2)}, u32[]{:S(2)}) async-start(f32[32,24,128]{2,1,0:T(8,128)} %sums.2), calls=%async_computation | async-start | bytes 786432 | tf_op jit(solution)/shard_map/all_to_all | solution.py:271
  17.2 0.6 pad_add_fusion.index_ref
  17.9 1.9 %own.1.own_ref = f32[3,16,128]{2,1,0:T(8,128)} custom-call(s32[2]{0:T(128)} %pad_add_fusion.index_ref, f32[2,8,8,512]{3,2,1,0:T(8,128)} %gains_ref.3, f32[2,8,8,512]{3,2,1,0:T(8,128)} %duals_ref.3, f32[4,8,8,512]{3,2,1,0:T(8,128)} %poly_ref.1), custom_call_target="tpu_custom_call" | custom-call | tf_op jit(solution)/shard_map/own/pallas_call | solution.py:178
  19.8 10.4 %all-to-all-done.arrived = f32[32,24,128]{2,1,0:T(8,128)S(1)} async-done(((f32[32,24,128]{2,1,0:T(8,128)}), f32[32,24,128]{2,1,0:T(8,128)S(1)}, u32[]{:S(2)}, u32[]{:S(2)}) %all-to-all-start) | async-done | bytes 393248 | tf_op jit(solution)/shard_map/all_to_all | solution.py:271
  30.2 0.0 copy-start.2
  30.2 0.7 copy-done.2
  31.0 1.8 %first.1 = f32[32,16,128]{2,1,0:T(8,128)} custom-call(f32[32,24,128]{2,1,0:T(8,128)} %copy-done.2, f32[3,16,128]{2,1,0:T(8,128)} %own.1.own_ref), custom_call_target="tpu_custom_call" | custom-call | tf_op jit(solution)/shard_map/first/pallas_call | solution.py:284
  32.8 17.5 %all_to_all.25.gains_ref = f32[32,16,128]{2,1,0:T(8,128)} all-to-all(f32[32,16,128]{2,1,0:T(8,128)} %first.1), channel_id=1, replica_groups=mesh['freq'=16,'tm'=32] {'tm'}, dimensions={0} | all-to-all | bytes 524288 | tf_op jit(solution)/shard_map/all_to_all | solution.py:271
  50.3 2.4 %sums.3 = f32[32,24,128]{2,1,0:T(8,128)} custom-call(f32[32,16,128]{2,1,0:T(8,128)} %all_to_all.25.gains_ref, bf16[2,8,8,128]{3,2,1,0:T(8,128)(2,1)} %coh_ref.3, f32[2,8,128]{2,1,0:T(8,128)} %vis_ref.3, s32[2,128]{1,0:T(2,128)} %pairs_ref.3), custom_call_target="tpu_custom_call" | custom-call | tf_op jit(solution)/shard_map/sums/pallas_call | solution.py:123
  52.7 5.7 %all-to-all-start.2 = ((f32[32,24,128]{2,1,0:T(8,128)}), f32[32,24,128]{2,1,0:T(8,128)S(1)}, u32[]{:S(2)}, u32[]{:S(2)}) async-start(f32[32,24,128]{2,1,0:T(8,128)} %sums.3), calls=%async_computation.2 | async-start | bytes 786432 | tf_op jit(solution)/shard_map/all_to_all | solution.py:271
  58.4 1.3 %slice_bitcast_fusion.gains_ref = f32[16,128]{1,0:T(8,128)} fusion(f32[32,16,128]{2,1,0:T(8,128)} %first.1), kind=kLoop, calls=%fused_computation | loop fusion | bytes 16384 | tf_op jit(solution)/shard_map/squeeze | solution.py:298
  59.7 11.6 %all-to-all-done.2.arrived = f32[32,24,128]{2,1,0:T(8,128)S(1)} async-done(((f32[32,24,128]{2,1,0:T(8,128)}), f32[32,24,128]{2,1,0:T(8,128)S(1)}, u32[]{:S(2)}, u32[]{:S(2)}) %all-to-all-start.2) | async-done | bytes 393248 | tf_op jit(solution)/shard_map/all_to_all | solution.py:271
  71.3 0.0 copy-start.1
  71.3 0.7 copy-done.1
  72.1 1.8 %last.1 = (f32[16,16,128]{2,1,0:T(8,128)}, f32[16,128]{1,0:T(8,128)}) custom-call(s32[2]{0:T(128)} %pad_add_fusion.index_ref, f32[32,24,128]{2,1,0:T(8,128)} %copy-done.1, f32[3,16,128]{2,1,0:T(8,128)} %own.1.own_ref, f32[16,128]{1,0:T(8,128)} %slice_bitcast_fusion.gains_ref), custom_call_target="tpu_custom_call" | custom-call | tf_op jit(solution)/shard_map/last/pallas_call | solution.py:292
  73.8 19.7 %all_to_all.26.arrived = f32[16,16,128]{2,1,0:T(8,128)} all-to-all(f32[16,16,128]{2,1,0:T(8,128)} %get-tuple-element.5), channel_id=1, replica_groups=mesh['freq'=16,'tm'=32] {'freq'}, dimensions={0} | all-to-all | bytes 262144 | tf_op jit(solution)/shard_map/all_to_all | solution.py:271
  93.6 1.8 %joined.1 = f32[32,32,128]{2,1,0:T(8,128)} custom-call(f32[16,16,128]{2,1,0:T(8,128)} %all_to_all.26.arrived, f32[16,128]{1,0:T(8,128)} %get-tuple-element.6.gains_ref), custom_call_target="tpu_custom_call" | custom-call | tf_op jit(solution)/shard_map/joined/pallas_call | solution.py:300
  95.3 19.9 %all_to_all.27 = f32[32,32,128]{2,1,0:T(8,128)S(1)} all-to-all(f32[32,32,128]{2,1,0:T(8,128)} %joined.1), channel_id=1, replica_groups=mesh['freq'=16,'tm'=32] {'tm'}, dimensions={0} | all-to-all | bytes 1048576 | tf_op jit(solution)/shard_map/all_to_all | solution.py:271
  115.3 4.5 %collective-permute-start = (f32[32,16,128]{2,1,0:T(8,128)S(1)}, f32[32,16,128]{2,1,0:T(8,128)S(1)}, u32[]{:S(2)}, u32[]{:S(2)}) collective-permute-start(f32[32,16,128]{2,1,0:T(8,128)S(1)} %slice.9), channel_id=1, source_target_pairs={{0,32},{32,0},{64,96},{96,64},{128,160},{160,128},{192,224},{224,1... | collective-permute-start | bytes 786440 | tf_op jit(solution)/shard_map/ppermute | solution.py:306
  119.8 1.1 collective-permute-done
  120.9 0.0 copy-done
  120.9 0.7 copy-done.3
  121.6 2.6 %end.1 = (f32[2,8,8,512]{3,2,1,0:T(8,128)}, f32[2,8,8,512]{3,2,1,0:T(8,128)}, f32[4,8,8,512]{3,2,1,0:T(8,128)}) custom-call(s32[2]{0:T(128)} %pad_add_fusion.index_ref, f32[1024,128]{1,0:T(8,128)} %bitcast.6, f32[512,128]{1,0:T(8,128)} %bitcast.7, f32[2,8,8,512]{3,2,1,0:T(8,128)} %duals_ref.3), custom_call_target="tpu_custom_call" | custom-call | tf_op jit(solution)/shard_map/end/pallas_call | solution.py:308
  (3 shorter events, 0.0 us)
Async XLA Ops:
  3.0 27.3 %all-to-all-start = ((f32[32,24,128]{2,1,0:T(8,128)}), f32[32,24,128]{2,1,0:T(8,128)S(1)}, u32[]{:S(2)}, u32[]{:S(2)}) async-start(f32[32,24,128]{2,1,0:T(8,128)} %sums.2), calls=%async_computation | async-start | bytes 786432 | tf_op jit(solution)/shard_map/all_to_all | solution.py:271
  30.2 0.7 copy-start.2
  52.7 18.6 %all-to-all-start.2 = ((f32[32,24,128]{2,1,0:T(8,128)}), f32[32,24,128]{2,1,0:T(8,128)S(1)}, u32[]{:S(2)}, u32[]{:S(2)}) async-start(f32[32,24,128]{2,1,0:T(8,128)} %sums.3), calls=%async_computation.2 | async-start | bytes 786432 | tf_op jit(solution)/shard_map/all_to_all | solution.py:271
  71.3 0.7 copy-start.1
  115.2 5.7 %copy-start = (f32[32,32,128]{2,1,0:T(8,128)}, f32[32,32,128]{2,1,0:T(8,128)S(1)}, u32[]{:S(2)}) copy-start(f32[32,32,128]{2,1,0:T(8,128)S(1)} %all_to_all.27) | copy-start | bytes 1572868
  115.3 5.7 %collective-permute-start = (f32[32,16,128]{2,1,0:T(8,128)S(1)}, f32[32,16,128]{2,1,0:T(8,128)S(1)}, u32[]{:S(2)}, u32[]{:S(2)}) collective-permute-start(f32[32,16,128]{2,1,0:T(8,128)S(1)} %slice.9), channel_id=1, source_target_pairs={{0,32},{32,0},{64,96},{96,64},{128,160},{160,128},{192,224},{224,1... | collective-permute-start | bytes 786440 | tf_op jit(solution)/shard_map/ppermute | solution.py:306
  120.9 0.7 copy-start.3
where the time goes:
time: 125 us; the launch traced here: 124 us
  blocking collectives  57.2 us (46%)
  starting transfers between devices  24.5 us (20%)
  waiting for transfers between devices  23.2 us (19%)
  Pallas kernels  14.5 us (12%)
  local copies, waits for them, and re-layouts  3.51 us (3%)
    all_to_all x3, blocking collectives, exchanged(): return lax.all_to_all(x, axis, split_axis=0, concat_axis=0, tiled=True)  57.2 us
    all_to_all x2, waiting for transfers between devices, exchanged(): return lax.all_to_all(x, axis, split_axis=0, concat_axis=0, tiled=True)  22.1 us
    all_to_all x2, starting transfers between devices, exchanged(): return lax.all_to_all(x, axis, split_axis=0, concat_axis=0, tiled=True)  20 us
    pallas_call x2, Pallas kernels, share_sums(): pl.pallas_call(functools.partial(sums_kernel, gathered), out_shape=jax.Sh...  4.7 us
    ppermute x1, starting transfers between devices, shards(): lax.ppermute(everything[:, 16:], 'freq', [(i, i ^ 1) for i in range(freqs)])  4.52 us
    pallas_call x1, Pallas kernels, shards(): pl.pallas_call(functools.partial(end_kernel, count), out_shape=(jax.Shape...  2.64 us
  transfers between devices with their start and end apart: 3, of which 3 were waited for; matrix products, arithmetic and copies ran while one was open for 2% of the time, Pallas kernels for 2%

commit v1 on v0

--- a/solution.py
+++ b/solution.py
@@ -58,6 +58,28 @@
     station = lax.broadcasted_iota(jnp.int32, (STATIONS, ROWS), 0)
     marks = [jnp.where(station == pairs_ref[i : i + 1, :], 1.0, 0.0) for i in range(2)]
     return jnp.concatenate(marks, axis=1).astype(BF16)
+
+
+SMEM = pl.BlockSpec(memory_space=pltpu.SMEM)
+VMEM = pl.BlockSpec(memory_space=pltpu.VMEM)
+
+def call(kernel, outs, *args, scratch=(), fast=None, slow_outs=False, limit=12 << 20, name=None):
+    fast = range(len(args)) if fast is None else fast
+    args = [
+        pltpu.with_memory_space_constraint(a, pltpu.MemorySpace.VMEM) if n in fast else a
+        for n, a in enumerate(args)
+    ]
+    kind = (lambda shape: jax.ShapeDtypeStruct(shape, F32)) if slow_outs else (lambda shape: pltpu.VMEM(shape, F32))
+    many = isinstance(outs, list)
+    return pl.pallas_call(
+        kernel,
+        out_shape=tuple(kind(o) for o in outs) if many else kind(outs),
+        in_specs=[SMEM if a.dtype == jnp.int32 and a.ndim == 1 else VMEM for a in args],
+        out_specs=tuple(VMEM for _ in outs) if many else VMEM,
+        scratch_shapes=list(scratch),
+        compiler_params=pltpu.CompilerParams(vmem_limit_bytes=limit),
+        name=name,
+    )(*args)
 
 
 def sums_kernel(gathered, gains_ref, coh_ref, vis_ref, pairs_ref, out_ref, at_p, at_q, terms_p, terms_q, summed):
@@ -120,10 +142,16 @@
 def share_sums(gains, coherencies, visibilities, pairs, gathered):
     rows = CHANS * 8 * DIRS
     terms = CHANS * 12 * DIRS
-    return pl.pallas_call(
+    return call(
         functools.partial(sums_kernel, gathered),
-        out_shape=jax.ShapeDtypeStruct((DIRS * CUTS, CHANS * 12, LANES), F32),
-        scratch_shapes=[
+        (DIRS * CUTS, CHANS * 12, LANES),
+        gains,
+        coherencies,
+        visibilities,
+        pairs,
+        fast=[0] if gathered else [],
+        limit=12 << 20 if gathered else 60 << 20,
+        scratch=[
             pltpu.VMEM((rows, ROWS), F32),
             pltpu.VMEM((rows, ROWS), F32),
             pltpu.VMEM((terms, ROWS), F32),
@@ -131,7 +159,7 @@
             pltpu.VMEM((CUTS, terms, LANES), F32),
         ],
         name="sums",
-    )(gains, coherencies, visibilities, pairs)
+    )
 
 
 def basis_of(channel, count):
@@ -168,19 +196,6 @@
             for j in range(1, POLY):
                 prior += basis[j] * poly_ref[j, i, :, lanes]
             out_ref[2, at, :] = row(prior)
-
-
-SMEM = pl.BlockSpec(memory_space=pltpu.SMEM)
-VMEM = pl.BlockSpec(memory_space=pltpu.VMEM)
-
-
-def own_share(index, gains, duals, poly, count):
-    return pl.pallas_call(
-        functools.partial(own_kernel, count),
-        out_shape=jax.ShapeDtypeStruct((3, CHANS * 8, LANES), F32),
-        in_specs=[SMEM, VMEM, VMEM, VMEM],
-        name="own",
-    )(index, gains, duals, poly)
 
 
 def both(ref, i, step):
@@ -213,7 +228,7 @@
         put[pl.ds(i, CHANS, stride=8), :] = gains[i] + step[i]
 
 
-def first_kernel(damping, arrived, own_ref, out_ref, sums_ref, new):
+def first_kernel(damping, arrived, own_ref, out_ref, new, sums_ref):
     updated(sums_ref, own_ref, own_ref.at[0], damping, arrived, new)
     value = new[...]
     for n in range(out_ref.shape[0]):
@@ -275,46 +290,52 @@
     freqs, times = lax.axis_size("freq"), lax.axis_size("tm")
     count = CHANS * freqs
     index = jnp.stack([lax.axis_index("freq"), lax.axis_index("tm")]).astype(jnp.int32)
-    share = jax.ShapeDtypeStruct((CHANS * 8, LANES), F32)
-    sums_scratch = pltpu.VMEM((CHANS * 12, LANES), F32)
-    new_scratch = pltpu.VMEM((CHANS * 8, LANES), F32)
-
-    own = own_share(index, gains_start, duals_start, poly_start, count)
+    share = (CHANS * 8, LANES)
+    scratch = [pltpu.VMEM((CHANS * 12, LANES), F32)]
+
+    own = call(
+        functools.partial(own_kernel, count),
+        (3, *share),
+        index,
+        gains_start,
+        duals_start,
+        poly_start,
+        fast=[],
+        name="own",
+    )
     sums = exchanged(share_sums(gains_start, coherencies, visibilities, pairs, False), "tm")
-    copies = pl.pallas_call(
-        functools.partial(first_kernel, 12.0),
-        out_shape=jax.ShapeDtypeStruct((times, CHANS * 8, LANES), F32),
-        scratch_shapes=[sums_scratch, new_scratch],
-        name="first",
-    )(sums, own)
+    copies, mine = call(
+        functools.partial(first_kernel, 12.0), [(times, *share), share], sums, own, scratch=scratch, name="first"
+    )
     gains = exchanged(copies, "tm")
     sums = exchanged(share_sums(gains, coherencies, visibilities, pairs, True), "tm")
-    fits, mine = pl.pallas_call(
+    fits, mine = call(
         functools.partial(last_kernel, 6.0, count, inverse_gram(count)),
-        out_shape=(jax.ShapeDtypeStruct((freqs, 16, LANES), F32), share),
-        in_specs=[SMEM, VMEM, VMEM, VMEM],
-        scratch_shapes=[sums_scratch],
+        [(freqs, 16, LANES), share],
+        index,
+        sums,
+        own,
+        mine,
+        fast=[1, 2, 3],
+        scratch=scratch,
         name="last",
-    )(index, sums, own, copies[0])
+    )
     fits = exchanged(fits, "freq")
-    copies = pl.pallas_call(
-        joined_kernel,
-        out_shape=jax.ShapeDtypeStruct((times, 32, LANES), F32),
-        name="joined",
-    )(fits, mine)
+    copies = call(joined_kernel, (times, 32, LANES), fits, mine, name="joined")
     everything = exchanged(copies, "tm")
     other = lax.ppermute(everything[:, 16:], "freq", [(i, i ^ 1) for i in range(freqs)])
     block = (CHANS, 8, DIRS, STATIONS)
-    return pl.pallas_call(
+    return call(
         functools.partial(end_kernel, count),
-        out_shape=(
-            jax.ShapeDtypeStruct(block, F32),
-            jax.ShapeDtypeStruct(block, F32),
-            jax.ShapeDtypeStruct((POLY, 8, DIRS, STATIONS), F32),
-        ),
-        in_specs=[SMEM, VMEM, VMEM, VMEM],
+        [block, block, (POLY, 8, DIRS, STATIONS)],
+        index,
+        everything.reshape(times * 32, LANES),
+        other.reshape(times * 16, LANES),
+        duals_start,
+        fast=[1, 2, 3],
+        slow_outs=True,
         name="end",
-    )(index, everything.reshape(times * 32, LANES), other.reshape(times * 16, LANES), duals_start)
+    )
 
 
 def solution(mesh):

time: 125 us -> 115 us (0.920)
  blocking collectives: 57.2 us -> 74.9 us
  waiting for transfers between devices: 23.2 us -> 13.4 us
  Pallas kernels: 14.5 us -> 6.41 us
  starting transfers between devices: 24.5 us -> 18.9 us
  local copies, waits for them, and re-layouts: 3.51 us -> 0.05 us
    all_to_all x3 -> x4, blocking collectives: 57.2 us -> 74.9 us  [exchanged(): return lax.all_to_all(x, axis, split_axis=0, concat_axis=0, tiled=True)]
    all_to_all x2 -> x1, waiting for transfers between devices: 22.1 us -> 12.3 us  [exchanged(): return lax.all_to_all(x, axis, split_axis=0, concat_axis=0, tiled=True)]
    pallas_call x7, Pallas kernels: 14.5 us -> 6.41 us  [call(): pl.pallas_call(kernel, out_shape=tuple((kind(o) for o in outs)) if many e...]
    all_to_all x2 -> x1, starting transfers between devices: 20 us -> 14.4 us  [exchanged(): return lax.all_to_all(x, axis, split_axis=0, concat_axis=0, tiled=True)]
    unnamed x8 -> x12, local copies, waits for them, and re-layouts: 2.2 us -> 0.03 us
    squeeze x1 -> x0, local copies, waits for them, and re-layouts: 1.3 us -> none  [shards(): copies[0]]
  transfers between devices with their start and end apart: 3 -> 2, of which waited for: 3 -> 2; matrix products, arithmetic and copies ran while one was open for 2% -> 0% of each run, Pallas kernels for 2% -> 1%
where the time goes in v1:
time: 115 us
  blocking collectives  74.9 us (65%)
  starting transfers between devices  18.9 us (16%)
  waiting for transfers between devices  13.4 us (12%)
  Pallas kernels  6.41 us (6%)
    all_to_all x4, blocking collectives, exchanged(): return lax.all_to_all(x, axis, split_axis=0, concat_axis=0, tiled=True)  74.9 us
    all_to_all x1, starting transfers between devices, exchanged(): return lax.all_to_all(x, axis, split_axis=0, concat_axis=0, tiled=True)  14.4 us
    all_to_all x1, waiting for transfers between devices, exchanged(): return lax.all_to_all(x, axis, split_axis=0, concat_axis=0, tiled=True)  12.3 us
    pallas_call x7, Pallas kernels, call(): pl.pallas_call(kernel, out_shape=tuple((kind(o) for o in outs)) if many e...  6.41 us
    ppermute x1, starting transfers between devices, shards(): lax.ppermute(everything[:, 16:], 'freq', [(i, i ^ 1) for i in range(freqs)])  4.51 us
  transfers between devices with their start and end apart: 2, of which 2 were waited for; matrix products, arithmetic and copies ran while one was open for 0% of the time, Pallas kernels for 1%

profile of v1, /device:TPU:1, one launch (start us, length us, event | category | flops | bytes accessed | tf_op | source)
XLA Modules:
  0.0 114.6 jit_solution(4609881382065750333)
XLA Ops:
  0.6 0.0 copy-start.2
  0.6 2.4 %sums.2 = f32[32,24,128]{2,1,0:T(8,128)} custom-call(f32[2,8,8,512]{3,2,1,0:T(8,128)} %gains_ref.3, bf16[2,8,8,128]{3,2,1,0:T(8,128)(2,1)} %coh_ref.3, f32[2,8,128]{2,1,0:T(8,128)} %vis_ref.3, s32[2,128]{1,0:T(2,128)} %pairs_ref.3), custom_call_target="tpu_custom_call" | custom-call | tf_op jit(solution)/shard_map/sums/pallas_call | solution.py:74
  3.0 14.4 %all-to-all-start = ((f32[32,24,128]{2,1,0:T(8,128)}), f32[32,24,128]{2,1,0:T(8,128)S(1)}, u32[]{:S(2)}, u32[]{:S(2)}) async-start(f32[32,24,128]{2,1,0:T(8,128)} %sums.2), calls=%async_computation | async-start | bytes 786432 | tf_op jit(solution)/shard_map/all_to_all | solution.py:286
  17.5 0.1 pad_add_fusion.index_ref
  17.5 0.0 copy-done.2
  17.5 0.0 copy-done
  17.5 0.0 copy-done.1
  17.5 0.6 own.1.own_ref
  18.2 12.3 %all-to-all-done.arrived = f32[32,24,128]{2,1,0:T(8,128)S(1)} async-done(((f32[32,24,128]{2,1,0:T(8,128)}), f32[32,24,128]{2,1,0:T(8,128)S(1)}, u32[]{:S(2)}, u32[]{:S(2)}) %all-to-all-start) | async-done | bytes 393248 | tf_op jit(solution)/shard_map/all_to_all | solution.py:286
  30.4 0.1 first.1
  30.5 0.0 copy-start.3
  30.5 0.0 copy-start.4
  30.6 0.0 copy-start.5
  30.6 17.3 %all_to_all.25.gains_ref = f32[32,16,128]{2,1,0:T(8,128)S(1)} all-to-all(f32[32,16,128]{2,1,0:T(8,128)S(1)} %get-tuple-element.7), channel_id=1, replica_groups=mesh['freq'=16,'tm'=32] {'tm'}, dimensions={0} | all-to-all | bytes 524288 | tf_op jit(solution)/shard_map/all_to_all | solution.py:286
  47.9 0.0 copy-done.3
  47.9 0.7 sums.3
  48.6 18.4 %all_to_all.26.arrived = f32[32,24,128]{2,1,0:T(8,128)S(1)} all-to-all(f32[32,24,128]{2,1,0:T(8,128)S(1)} %sums.3), channel_id=1, replica_groups=mesh['freq'=16,'tm'=32] {'tm'}, dimensions={0} | all-to-all | bytes 786432 | tf_op jit(solution)/shard_map/all_to_all | solution.py:286
  67.0 0.6 last.1
  67.7 19.4 %all_to_all.27.arrived = f32[16,16,128]{2,1,0:T(8,128)S(1)} all-to-all(f32[16,16,128]{2,1,0:T(8,128)S(1)} %get-tuple-element.9), channel_id=1, replica_groups=mesh['freq'=16,'tm'=32] {'freq'}, dimensions={0} | all-to-all | bytes 262144 | tf_op jit(solution)/shard_map/all_to_all | solution.py:286
  87.1 0.1 joined.1
  87.1 19.7 %all_to_all.28 = f32[32,32,128]{2,1,0:T(8,128)S(1)} all-to-all(f32[32,32,128]{2,1,0:T(8,128)S(1)} %joined.1), channel_id=1, replica_groups=mesh['freq'=16,'tm'=32] {'tm'}, dimensions={0} | all-to-all | bytes 1048576 | tf_op jit(solution)/shard_map/all_to_all | solution.py:286
  106.9 4.5 %collective-permute-start = (f32[32,16,128]{2,1,0:T(8,128)S(1)}, f32[32,16,128]{2,1,0:T(8,128)S(1)}, u32[]{:S(2)}, u32[]{:S(2)}) collective-permute-start(f32[32,16,128]{2,1,0:T(8,128)S(1)} %slice.4), channel_id=1, source_target_pairs={{0,32},{32,0},{64,96},{96,64},{128,160},{160,128},{192,224},{224,1... | collective-permute-start | bytes 786440 | tf_op jit(solution)/shard_map/ppermute | solution.py:326
  111.4 1.1 collective-permute-done
  112.6 2.0 %end.1 = (f32[2,8,8,512]{3,2,1,0:T(8,128)}, f32[2,8,8,512]{3,2,1,0:T(8,128)}, f32[4,8,8,512]{3,2,1,0:T(8,128)}) custom-call(s32[2]{0:T(128)S(1)} %pad_add_fusion.index_ref, f32[1024,128]{1,0:T(8,128)S(1)} %bitcast.4, f32[512,128]{1,0:T(8,128)S(1)} %bitcast.5, f32[2,8,8,512]{3,2,1,0:T(8,128)S(1)} %copy-done.1), custom_call_target="tpu_custom_call" | custom-call | tf_op jit(solution)/shard_map/end/pallas_call | solution.py:74
  (5 shorter events, 0.0 us)
Async XLA Ops:
  0.6 16.9 %copy-start.2 = (f32[4,8,8,512]{3,2,1,0:T(8,128)S(1)}, f32[4,8,8,512]{3,2,1,0:T(8,128)}, u32[]{:S(2)}) copy-start(f32[4,8,8,512]{3,2,1,0:T(8,128)} %poly_ref.1) | copy-start | bytes 1572868
  3.0 14.5 %copy-start = (f32[2,8,8,512]{3,2,1,0:T(8,128)S(1)}, f32[2,8,8,512]{3,2,1,0:T(8,128)}, u32[]{:S(2)}) copy-start(f32[2,8,8,512]{3,2,1,0:T(8,128)} %gains_ref.3) | copy-start | bytes 786436
  3.0 14.5 %copy-start.1 = (f32[2,8,8,512]{3,2,1,0:T(8,128)S(1)}, f32[2,8,8,512]{3,2,1,0:T(8,128)}, u32[]{:S(2)}) copy-start(f32[2,8,8,512]{3,2,1,0:T(8,128)} %duals_ref.3) | copy-start | bytes 786436
  3.0 27.4 %all-to-all-start = ((f32[32,24,128]{2,1,0:T(8,128)}), f32[32,24,128]{2,1,0:T(8,128)S(1)}, u32[]{:S(2)}, u32[]{:S(2)}) async-start(f32[32,24,128]{2,1,0:T(8,128)} %sums.2), calls=%async_computation | async-start | bytes 786432 | tf_op jit(solution)/shard_map/all_to_all | solution.py:286
  30.5 17.4 %copy-start.3 = (bf16[2,8,8,128]{3,2,1,0:T(8,128)(2,1)S(1)}, bf16[2,8,8,128]{3,2,1,0:T(8,128)(2,1)}, u32[]{:S(2)}) copy-start(bf16[2,8,8,128]{3,2,1,0:T(8,128)(2,1)} %coh_ref.3) | copy-start | bytes 98308
  30.5 17.4 %copy-start.4 = (f32[2,8,128]{2,1,0:T(8,128)S(1)}, f32[2,8,128]{2,1,0:T(8,128)}, u32[]{:S(2)}) copy-start(f32[2,8,128]{2,1,0:T(8,128)} %vis_ref.3) | copy-start | bytes 24580
  30.6 17.4 %copy-start.5 = (s32[2,128]{1,0:T(2,128)S(1)}, s32[2,128]{1,0:T(2,128)}, u32[]{:S(2)}) copy-start(s32[2,128]{1,0:T(2,128)} %pairs_ref.3) | copy-start | bytes 3076
  106.9 5.7 %collective-permute-start = (f32[32,16,128]{2,1,0:T(8,128)S(1)}, f32[32,16,128]{2,1,0:T(8,128)S(1)}, u32[]{:S(2)}, u32[]{:S(2)}) collective-permute-start(f32[32,16,128]{2,1,0:T(8,128)S(1)} %slice.4), channel_id=1, source_target_pairs={{0,32},{32,0},{64,96},{96,64},{128,160},{160,128},{192,224},{224,1... | collective-permute-start | bytes 786440 | tf_op jit(solution)/shard_map/ppermute | solution.py:326

commit v2 on v1

v2 whole, which is shorter than its diff:
```python
import functools

import jax
import jax.numpy as jnp
import numpy as np
from jax import lax
from jax.experimental import pallas as pl
from jax.experimental.pallas import tpu as pltpu
from jax.sharding import Mesh
from jax.sharding import PartitionSpec as P

ITERS = 2
RHO = 16.0
CHANS = 2
DIRS = 8
STATIONS = 512
ROWS = 128
POLY = 4
LANES = 128
CUTS = STATIONS // LANES
GROUPS = 4
PAIR = DIRS // GROUPS
SOURCES = CHANS * GROUPS
F32 = jnp.float32
BF16 = jnp.bfloat16


def adjoint(matrix):
    re, im = matrix
    return ([re[0], re[2], re[1], re[3]], [-im[0], -im[2], -im[1], -im[3]])


def product(left, right):
    lr, li = left
    rr, ri = right
    out_re, out_im = [], []
    for row in range(2):
        for col in range(2):
            a = 2 * row
            out_re.append(lr[a] * rr[col] - li[a] * ri[col] + lr[a + 1] * rr[col + 2] - li[a + 1] * ri[col + 2])
            out_im.append(lr[a] * ri[col] + li[a] * rr[col] + lr[a + 1] * ri[col + 2] + li[a + 1] * rr[col + 2])
    return (out_re, out_im)


def normal(matrix):
    re, im = matrix
    return [
        re[0] ** 2 + im[0] ** 2 + re[1] ** 2 + im[1] ** 2,
        re[2] ** 2 + im[2] ** 2 + re[3] ** 2 + im[3] ** 2,
        re[0] * re[2] + im[0] * im[2] + re[1] * re[3] + im[1] * im[3],
        im[0] * re[2] - re[0] * im[2] + im[1] * re[3] - re[1] * im[3],
    ]


def two_parts(x):
    high = x.astype(BF16)
    low = (x - high.astype(F32)).astype(BF16)
    return jnp.concatenate([high, low], axis=0)


SMEM = pl.BlockSpec(memory_space=pltpu.SMEM)
VMEM = pl.BlockSpec(memory_space=pltpu.VMEM)

def call(kernel, outs, *args, scratch=(), fast=None, kinds=None, slow_outs=False, limit=12 << 20, name=None):
    fast = range(len(args)) if fast is None else fast
    args = [
        pltpu.with_memory_space_constraint(a, pltpu.MemorySpace.VMEM) if n in fast else a
        for n, a in enumerate(args)
    ]
    kind = jax.ShapeDtypeStruct if slow_outs else pltpu.VMEM
    many = isinstance(outs, list)
    kinds = kinds or [F32] * len(outs)
    return pl.pallas_call(
        kernel,
        out_shape=tuple(kind(o, t) for o, t in zip(outs, kinds)) if many else kind(outs, F32),
        in_specs=[SMEM if a.dtype == jnp.int32 and a.ndim == 1 else VMEM for a in args],
        out_specs=tuple(VMEM for _ in outs) if many else VMEM,
        scratch_shapes=list(scratch),
        compiler_params=pltpu.CompilerParams(vmem_limit_bytes=limit),
        name=name,
    )(*args)


def basis_of(channel, count):
    x = (2.0 * channel.astype(F32) + 1.0) / count - 1.0
    return [1.0 + 0.0 * x, x, 1.5 * x * x - 0.5, 2.5 * x * x * x - 1.5 * x]


def inverse_gram(count):
    x = (2.0 * np.arange(count) + 1.0) / count - 1.0
    basis = np.stack([np.ones_like(x), x, 1.5 * x * x - 0.5, 2.5 * x**3 - 1.5 * x], axis=1)
    return np.linalg.inv(basis.T @ basis)


def weights_of(basis, gram):
    return [sum(float(gram[j, i]) * basis[i] for i in range(POLY)) for j in range(POLY)]


def split(parts):
    return (parts[:4], parts[4:])


def flat(matrix):
    return matrix[0] + matrix[1]


def pack_kernel(gains_ref, coh_ref, vis_ref, pairs_ref, out_ref, sky):
    station = lax.broadcasted_iota(jnp.int32, (STATIONS, ROWS), 0)
    hot = [jnp.where(station == pairs_ref[i : i + 1, :], 1.0, 0.0) for i in range(2)]
    hot = jnp.concatenate(hot, axis=1).astype(BF16)
    rows = gains_ref[...].reshape(CHANS * 8 * DIRS, STATIONS)
    found = jnp.dot(two_parts(rows), hot, preferred_element_type=F32)
    found = found[: rows.shape[0]] + found[rows.shape[0] :]
    names = jnp.concatenate(
        [pairs_ref[0:2, :].astype(F32), jnp.zeros((6, ROWS), F32)],
        axis=0,
    )
    for c in range(CHANS):
        at = [found[(c * 8 + i) * DIRS : (c * 8 + i + 1) * DIRS] for i in range(8)]
        first = split([a[:, :ROWS] for a in at])
        second = split([a[:, ROWS:] for a in at])
        parts = [coh_ref[c, i].astype(F32) for i in range(8)]
        for i in range(8):
            sky[c, pl.ds(i * DIRS, DIRS), :] = parts[i]
        model = flat(product(product(first, split(parts)), adjoint(second)))
        rest = vis_ref[c] - jnp.concatenate([jnp.sum(m, axis=0, keepdims=True) for m in model], axis=0)
        for g in range(GROUPS):
            for d in range(PAIR):
                out_ref[c * GROUPS + g, pl.ds(d * 8, 8), :] = sky[c, pl.ds(d * GROUPS + g, 8, stride=DIRS), :]
            out_ref[c * GROUPS + g, pl.ds(16, 8), :] = rest
            out_ref[c * GROUPS + g, pl.ds(24, 8), :] = names


def own_kernel(count, index_ref, gains_ref, duals_ref, poly_ref, out_ref):
    freq, c, g = index_ref[0], index_ref[1], index_ref[2]
    basis = basis_of(freq * CHANS + c, count)
    sublane = lax.broadcasted_iota(jnp.int32, (DIRS, STATIONS), 0)
    for i in range(8):
        prior = basis[0] * poly_ref[0, i]
        for j in range(1, POLY):
            prior += basis[j] * poly_ref[j, i]
        for n, tile in enumerate((gains_ref[c, i], duals_ref[c, i], prior)):
            for d in range(PAIR):
                row = jnp.sum(jnp.where(sublane == d * GROUPS + g, tile, 0.0), axis=0, keepdims=True)
                for q in range(CUTS):
                    out_ref[n, pl.ds(i * 8 + q * PAIR + d, 1), :] = row[:, q * LANES : (q + 1) * LANES]


def looked_up(gains_ref, hot_ref, at_ref):
    rows = jnp.concatenate(
        [
            jnp.concatenate(
                [gains_ref[pl.ds(q * PAIR + d, 8, stride=8), :] for q in range(CUTS)], axis=1
            )
            for d in range(PAIR)
        ],
        axis=0,
    )
    found = jnp.dot(two_parts(rows), hot_ref[...], preferred_element_type=F32)
    found = found[:16] + found[16:]
    for b in range(2 * SOURCES):
        at_ref[pl.ds(b * 16, 16), :] = found[:, b * ROWS : (b + 1) * ROWS]


def ends(at_ref, d):
    first = [at_ref[pl.ds(d * 8 + i, SOURCES, stride=16), :] for i in range(8)]
    second = [at_ref[pl.ds(SOURCES * 16 + d * 8 + i, SOURCES, stride=16), :] for i in range(8)]
    return split(first), split(second)


def sky_of(rows_ref, d):
    return split([rows_ref[pl.ds(d * 8 + i, SOURCES, stride=32), :] for i in range(8)])


def summed(rest, rows_ref, at_ref, hot_ref, out_ref, terms, total_ref):
    half = SOURCES * 24
    for d in range(PAIR):
        first, second = ends(at_ref, d)
        sky = sky_of(rows_ref, d)
        left = product(first, sky)
        right = product(sky, adjoint(second))
        ahead = flat(product(rest, adjoint(right))) + normal(right)
        behind = flat(product(adjoint(rest), left)) + normal(adjoint(left))
        for i in range(12):
            terms[pl.ds(d * 12 + i, SOURCES, stride=24), :] = ahead[i]
            terms[pl.ds(half + d * 12 + i, SOURCES, stride=24), :] = behind[i]
    wide = jnp.concatenate([terms[pl.ds(b * 24, 24), :] for b in range(2 * SOURCES)], axis=1)
    total = lax.dot_general(
        two_parts(wide), hot_ref[...], (((1,), (1,)), ((), ())), preferred_element_type=F32
    )
    total = total[:24] + total[24:]
    for q in range(CUTS):
        total_ref[q] = total[:, q * LANES : (q + 1) * LANES]
    for q in range(CUTS):
        for d in range(PAIR):
            part = total_ref[q, pl.ds(d * 12, 12), :]
            for n in range(out_ref.shape[0]):
                out_ref[n, pl.ds(q * PAIR + d, 12, stride=8), :] = part


def model_of(rows_ref, at_ref):
    model = None
    for d in range(PAIR):
        first, second = ends(at_ref, d)
        part = flat(product(product(first, sky_of(rows_ref, d)), adjoint(second)))
        model = part if model is None else [a + b for a, b in zip(model, part)]
    return model


def start_kernel(rows_ref, own_ref, out_ref, hot_ref, model_ref, at, terms, total):
    station = lax.broadcasted_iota(jnp.int32, (STATIONS, ROWS), 0).astype(F32)
    for end in range(2):
        for n in range(SOURCES):
            name = rows_ref[pl.ds(n * 32 + 24 + end, 1), :]
            lanes = pl.ds((end * SOURCES + n) * ROWS, ROWS)
            hot_ref[:, lanes] = jnp.where(station == name, 1.0, 0.0).astype(BF16)
    looked_up(own_ref.at[0], hot_ref, at)
    rest = split([rows_ref[pl.ds(16 + i, SOURCES, stride=32), :] for i in range(8)])
    summed(rest, rows_ref, at, hot_ref, out_ref, terms, total)
    model = model_of(rows_ref, at)
    for i in range(8):
        model_ref[pl.ds(i * 8, 8), :] = model[i]


def stepped(arrived, gains_ref, own_ref, damping, put):
    total = []
    for i in range(12):
        value = arrived[0, pl.ds(i * 8, 8), :]
        for n in range(1, arrived.shape[0]):
            value = value + arrived[n, pl.ds(i * 8, 8), :]
        total.append(value)
    tile = lambda ref, i: ref[pl.ds(i * 8, 8), :]
    gains = [tile(gains_ref, i) for i in range(8)]
    way = [
        total[i] - tile(own_ref.at[1], i) - RHO * (gains[i] - tile(own_ref.at[2], i)) for i in range(8)
    ]
    top, bottom, cross_re, cross_im = total[8:]
    shift = damping * 0.5 * (top + bottom) + RHO
    upper = top + shift
    lower = bottom + shift
    scale = 1.0 / (upper * lower - cross_re * cross_re - cross_im * cross_im)
    zeros = jnp.zeros_like(scale)
    inverse = (
        [lower * scale, -cross_re * scale, -cross_re * scale, upper * scale],
        [zeros, -cross_im * scale, cross_im * scale, zeros],
    )
    step = flat(product(split(way), inverse))
    new = [gains[i] + step[i] for i in range(8)]
    for i in range(8):
        put[pl.ds(i * 8, 8), :] = new[i]
    return new


def middle_kernel(damping, arrived, own_ref, rows_ref, hot_ref, model_ref, out_ref, gains_ref, at_ref):
    stepped(arrived, own_ref.at[0], own_ref, damping, gains_ref)
    looked_up(gains_ref, hot_ref, at_ref)
    model = model_of(rows_ref, at_ref)
    for i in range(8):
        change = model_ref[pl.ds(i * 8, 8), :] - model[i]
        for n in range(out_ref.shape[0]):
            out_ref[n, pl.ds(i * 8, 8), :] = change


def second_kernel(arrived, rows_ref, hot_ref, at_ref, out_ref, terms, total):
    rest = []
    for i in range(8):
        value = rows_ref[pl.ds(16 + i, SOURCES, stride=32), :]
        for n in range(arrived.shape[0]):
            value = value + arrived[n, pl.ds(i * 8, 8), :]
        rest.append(value)
    summed(split(rest), rows_ref, at_ref, hot_ref, out_ref, terms, total)


def last_kernel(damping, count, gram, index_ref, arrived, gains_ref, own_ref, fit_ref, mine_ref, new):
    gains = stepped(arrived, gains_ref, own_ref, damping, new)
    freq, c, q = index_ref[0], index_ref[1], index_ref[3]
    weights = weights_of(basis_of(freq * CHANS + c, count), gram)

    def own_cut(tile):
        chosen = tile[:PAIR]
        for n in range(1, CUTS):
            chosen = jnp.where(q == n, tile[n * PAIR : (n + 1) * PAIR], chosen)
        return chosen

    mine_ref[...] = jnp.concatenate([own_cut(g) for g in gains], axis=0)
    mixed = jnp.concatenate(
        [own_cut(gains[i] + own_ref[1, pl.ds(i * 8, 8), :] / RHO) for i in range(8)], axis=0
    )
    for n in range(fit_ref.shape[0]):
        fit_ref[n] = weights[n % POLY] * mixed


def joined_kernel(arrived, gains_ref, out_ref):
    total = arrived[0]
    for n in range(1, arrived.shape[0]):
        total = total + arrived[n]
    gains = gains_ref[...]
    for n in range(out_ref.shape[0]):
        out_ref[n, pl.ds(0, 16), :] = gains
        out_ref[n, pl.ds(16, 16), :] = total


def end_kernel(count, index_ref, all_ref, other_ref, duals_ref, gains_out, duals_out, poly_out):
    freq = index_ref[0]
    core = freq % 2
    basis = [basis_of(freq * CHANS + c, count) for c in range(CHANS)]
    mine = [[jnp.where(core == 0, basis[c][j], basis[c][j + 2]) for j in range(2)] for c in range(CHANS)]
    his = [[jnp.where(core == 0, basis[c][j + 2], basis[c][j]) for j in range(2)] for c in range(CHANS)]

    def tile(ref, c, q, row, size):
        place = c * 16 + (q // 2) * 8 + q % 2
        return jnp.concatenate(
            [ref[pl.ds(place * size + row + d, GROUPS, stride=2 * size), :] for d in range(PAIR)], axis=0
        )

    for i in range(8):
        for q in range(CUTS):
            lanes = pl.ds(q * LANES, LANES)
            own = [tile(all_ref, c, q, 16 + i * PAIR, 32) for c in range(CHANS)]
            far = [tile(other_ref, c, q, i * PAIR, 16) for c in range(CHANS)]
            for j in range(2):
                poly_out[2 * core + j, i, :, lanes] = own[j]
                poly_out[2 - 2 * core + j, i, :, lanes] = far[j]
            for c in range(CHANS):
                gains = tile(all_ref, c, q, i * PAIR, 32)
                gains_out[c, i, :, lanes] = gains
                prior = mine[c][0] * own[0] + mine[c][1] * own[1] + his[c][0] * far[0] + his[c][1] * far[1]
                duals_out[c, i, :, lanes] = duals_ref[c, i, :, lanes] + RHO * (gains - prior)


def exchanged(x, axis):
    return lax.all_to_all(x, axis, split_axis=0, concat_axis=0, tiled=True)


TIMES = ("c", "r1", "g", "r0")


def shards(visibilities, coherencies, pairs, gains_start, duals_start, poly_start):
    freqs = lax.axis_size("freq")
    times = lax.axis_size(TIMES)
    count = CHANS * freqs
    index = jnp.stack(
        [lax.axis_index("freq"), lax.axis_index("c"), lax.axis_index("g"), lax.axis_index(("r1", "r0"))]
    ).astype(jnp.int32)
    sums_shape = (CUTS, 12 * 8, LANES)
    tiles = (64, LANES)
    share = (16, LANES)
    work = [pltpu.VMEM((2 * SOURCES * 24, ROWS), F32), pltpu.VMEM((CUTS, 24, LANES), F32)]

    sent = call(
        pack_kernel,
        (SOURCES, 32, ROWS),
        gains_start,
        coherencies,
        visibilities,
        pairs,
        fast=[],
        limit=60 << 20,
        scratch=[pltpu.VMEM((CHANS, 64, ROWS), F32)],
        name="pack",
    )
    own = call(
        functools.partial(own_kernel, count), (3, *tiles), index, gains_start, duals_start, poly_start, fast=[], name="own"
    )
    rows = exchanged(sent, ("c", "g")).reshape(SOURCES * 32, ROWS)
    sums, hot, model = call(
        start_kernel,
        [sums_shape, (STATIONS, 2 * SOURCES * ROWS), tiles],
        rows,
        own,
        kinds=[F32, BF16, F32],
        scratch=[pltpu.VMEM((2 * SOURCES * 16, ROWS), F32), *work],
        name="start",
    )
    sums = exchanged(sums, ("r1", "r0"))
    change, gains, at = call(
        functools.partial(middle_kernel, 12.0),
        [(GROUPS, *tiles), tiles, (2 * SOURCES * 16, ROWS)],
        sums,
        own,
        rows,
        hot,
        model,
        name="middle",
    )
    change = exchanged(change, "g")
    sums = call(second_kernel, sums_shape, change, rows, hot, at, scratch=work, name="second")
    sums = exchanged(sums, ("r1", "r0"))
    fits, mine = call(
        functools.partial(last_kernel, 6.0, count, inverse_gram(count)),
        [(freqs * CHANS, *share), share],
        index,
        sums,
        gains,
        own,
        fast=[1, 2, 3],
        scratch=[pltpu.VMEM(tiles, F32)],
        name="last",
    )
    fits = exchanged(fits, ("freq", "c"))
    copies = call(joined_kernel, (times, 32, LANES), fits, mine, name="joined")
    everything = exchanged(copies, TIMES)
    other = lax.ppermute(everything[:, 16:], "freq", [(i, i ^ 1) for i in range(freqs)])
    block = (CHANS, 8, DIRS, STATIONS)
    return call(
        functools.partial(end_kernel, count),
        [block, block, (POLY, 8, DIRS, STATIONS)],
        index,
        everything.reshape(times * 32, LANES),
        other.reshape(times * 16, LANES),
        duals_start,
        fast=[1, 2, 3],
        slow_outs=True,
        name="end",
    )


def solution(mesh):
    freqs = mesh.shape["freq"]
    fine = Mesh(mesh.devices.reshape(freqs, CHANS, 2, GROUPS, 2), ("freq", *TIMES))
    placed = (
        P("freq", None, TIMES),
        P("freq", None, None, TIMES),
        P(None, TIMES),
        P("freq", None, None, None),
        P("freq", None, None, None),
        P(),
    )
    return jax.shard_map(
        shards,
        mesh=fine,
        in_specs=placed,
        out_specs=(P("freq", None, None, None), P("freq", None, None, None), P()),
        check_vma=False,
    )
```

time: 115 us -> 105 us (0.913)
  waiting for transfers between devices: 13.4 us -> 6.53 us
  blocking collectives: 74.9 us -> 68.3 us
  local copies, waits for them, and re-layouts: 0.05 us -> 2.97 us
  Pallas kernels: 6.41 us -> 8.36 us
  starting transfers between devices: 18.9 us -> 17.7 us
    all_to_all x1, waiting for transfers between devices: 12.3 us -> 5.39 us  [exchanged(): return lax.all_to_all(x, axis, split_axis=0, concat_axis=0, tiled=True)]
    all_to_all x4 -> x5, blocking collectives: 74.9 us -> 68.3 us  [exchanged(): return lax.all_to_all(x, axis, split_axis=0, concat_axis=0, tiled=True)]
    unnamed x12 -> x8, local copies, waits for them, and re-layouts: 0.03 us -> 2.95 us
    pallas_call x7 -> x8, Pallas kernels: 6.41 us -> 8.36 us  [call(): pl.pallas_call(kernel, out_shape=tuple((kind(o, t) for o, t in zip(outs,...]
    all_to_all x1, starting transfers between devices: 14.4 us -> 12.9 us  [exchanged(): return lax.all_to_all(x, axis, split_axis=0, concat_axis=0, tiled=True)]
where the time goes in v2:
time: 105 us
  blocking collectives  68.3 us (65%)
  starting transfers between devices  17.7 us (17%)
  Pallas kernels  8.36 us (8%)
  waiting for transfers between devices  6.53 us (6%)
  local copies, waits for them, and re-layouts  2.97 us (3%)
    all_to_all x5, blocking collectives, exchanged(): return lax.all_to_all(x, axis, split_axis=0, concat_axis=0, tiled=True)  68.3 us
    all_to_all x1, starting transfers between devices, exchanged(): return lax.all_to_all(x, axis, split_axis=0, concat_axis=0, tiled=True)  12.9 us
    pallas_call x8, Pallas kernels, call(): pl.pallas_call(kernel, out_shape=tuple((kind(o, t) for o, t in zip(outs,...  8.36 us
    all_to_all x1, waiting for transfers between devices, exchanged(): return lax.all_to_all(x, axis, split_axis=0, concat_axis=0, tiled=True)  5.39 us
    ppermute x1, starting transfers between devices, shards(): lax.ppermute(everything[:, 16:], 'freq', [(i, i ^ 1) for i in range(freqs)])  4.81 us
    unnamed x8, local copies, waits for them, and re-layouts  2.95 us
  transfers between devices with their start and end apart: 2, of which 2 were waited for; matrix products, arithmetic and copies ran while one was open for 0% of the time, Pallas kernels for 1%

profile of v2, /device:TPU:1, one launch (start us, length us, event | category | flops | bytes accessed | tf_op | source)
XLA Modules:
  0.0 104.6 jit_solution(4230562808828335958)
XLA Ops:
  0.6 1.9 %pack.1 = f32[8,32,128]{2,1,0:T(8,128)} custom-call(f32[2,8,8,512]{3,2,1,0:T(8,128)} %gains_ref.3, bf16[2,8,8,128]{3,2,1,0:T(8,128)(2,1)} %coh_ref.1, f32[2,8,128]{2,1,0:T(8,128)} %vis_ref.1, s32[2,128]{1,0:T(2,128)} %pairs_ref.1), custom_call_target="tpu_custom_call" | custom-call | tf_op jit(solution)/shard_map/pack/pallas_call | solution.py:73
  2.5 12.9 %all-to-all-start = ((f32[8,32,128]{2,1,0:T(8,128)}), f32[8,32,128]{2,1,0:T(8,128)S(1)}, u32[]{:S(2)}, u32[]{:S(2)}) async-start(f32[8,32,128]{2,1,0:T(8,128)} %pack.1), calls=%async_computation | async-start | bytes 262144 | tf_op jit(solution)/shard_map/all_to_all | solution.py:332
  15.4 0.1 pad_add_fusion.index_ref
  15.5 0.0 copy-start
  15.5 0.9 copy-done
  16.4 0.9 copy-done.1
  17.4 1.0 copy-done.3
  18.4 0.8 own.1.own_ref
  19.2 5.4 %all-to-all-done = f32[8,32,128]{2,1,0:T(8,128)S(1)} async-done(((f32[8,32,128]{2,1,0:T(8,128)}), f32[8,32,128]{2,1,0:T(8,128)S(1)}, u32[]{:S(2)}, u32[]{:S(2)}) %all-to-all-start) | async-done | bytes 131104 | tf_op jit(solution)/shard_map/all_to_all | solution.py:332
  24.6 1.7 %start.1 = (f32[4,96,128]{2,1,0:T(8,128)S(1)}, bf16[512,2048]{1,0:T(8,128)(2,1)S(1)}, f32[64,128]{1,0:T(8,128)S(1)}) custom-call(f32[256,128]{1,0:T(8,128)S(1)} %bitcast.8, f32[3,64,128]{2,1,0:T(8,128)S(1)} %own.1.own_ref), custom_call_target="tpu_custom_call" | custom-call | tf_op jit(solution)/shard_map/start/pallas_call | solution.py:73
  26.3 7.4 %all_to_all.30.arrived = f32[4,96,128]{2,1,0:T(8,128)S(1)} all-to-all(f32[4,96,128]{2,1,0:T(8,128)S(1)} %get-tuple-element.11), channel_id=1, replica_groups=mesh['freq'=16,'c'=2,'r1'=2,'g'=4,'r0'=2] {'r1','r0'}, dimensions={0} | all-to-all | bytes 393216 | tf_op jit(solution)/shard_map/all_to_all | solution.py:332
  33.6 0.5 middle.1
  34.2 9.6 %all_to_all.31.arrived = f32[4,64,128]{2,1,0:T(8,128)S(1)} all-to-all(f32[4,64,128]{2,1,0:T(8,128)S(1)} %get-tuple-element.14), channel_id=1, replica_groups=mesh['freq'=16,'c'=2,'r1'=2,'g'=4,'r0'=2] {'g'}, dimensions={0} | all-to-all | bytes 262144 | tf_op jit(solution)/shard_map/all_to_all | solution.py:332
  43.8 0.8 second.1
  44.6 0.0 copy-start.2
  44.6 6.9 %all_to_all.32.arrived = f32[4,96,128]{2,1,0:T(8,128)S(1)} all-to-all(f32[4,96,128]{2,1,0:T(8,128)S(1)} %second.1), channel_id=1, replica_groups=mesh['freq'=16,'c'=2,'r1'=2,'g'=4,'r0'=2] {'r1','r0'}, dimensions={0} | all-to-all | bytes 393216 | tf_op jit(solution)/shard_map/all_to_all | solution.py:332
  51.5 0.6 last.1
  52.1 25.4 %all_to_all.33.arrived = f32[32,16,128]{2,1,0:T(8,128)S(1)} all-to-all(f32[32,16,128]{2,1,0:T(8,128)S(1)} %get-tuple-element.17), channel_id=1, replica_groups=mesh['freq'=16,'c'=2,'r1'=2,'g'=4,'r0'=2] {'freq','c'}, dimensions={0} | all-to-all | bytes 524288 | tf_op jit(solution)/shard_map/all_to_all | solution.py:332
  77.6 0.1 joined.1
  77.6 19.0 %all_to_all.34 = f32[32,32,128]{2,1,0:T(8,128)S(1)} all-to-all(f32[32,32,128]{2,1,0:T(8,128)S(1)} %joined.1), channel_id=1, replica_groups=mesh['freq'=16,'c'=2,'r1'=2,'g'=4,'r0'=2] {'c','r1','g','r0'}, dimensions={0} | all-to-all | bytes 1048576 | tf_op jit(solution)/shard_map/all_to_all | solution.py:332
  96.6 4.8 %collective-permute-start = (f32[32,16,128]{2,1,0:T(8,128)S(1)}, f32[32,16,128]{2,1,0:T(8,128)S(1)}, u32[]{:S(2)}, u32[]{:S(2)}) collective-permute-start(f32[32,16,128]{2,1,0:T(8,128)S(1)} %slice.4), channel_id=1, source_target_pairs={{0,32},{32,0},{64,96},{96,64},{128,160},{160,128},{192,224},{224,1... | collective-permute-start | bytes 786440 | tf_op jit(solution)/shard_map/ppermute | solution.py:403
  101.4 1.1 %collective-permute-done = f32[32,16,128]{2,1,0:T(8,128)S(1)} collective-permute-done((f32[32,16,128]{2,1,0:T(8,128)S(1)}, f32[32,16,128]{2,1,0:T(8,128)S(1)}, u32[]{:S(2)}, u32[]{:S(2)}) %collective-permute-start) | collective-permute-done | bytes 262176 | tf_op jit(solution)/shard_map/ppermute | solution.py:403
  102.6 0.0 copy-done.2
  102.6 2.0 %end.1 = (f32[2,8,8,512]{3,2,1,0:T(8,128)}, f32[2,8,8,512]{3,2,1,0:T(8,128)}, f32[4,8,8,512]{3,2,1,0:T(8,128)}) custom-call(s32[4]{0:T(128)S(1)} %pad_add_fusion.index_ref, f32[1024,128]{1,0:T(8,128)S(1)} %bitcast.7, f32[512,128]{1,0:T(8,128)S(1)} %bitcast.11, f32[2,8,8,512]{3,2,1,0:T(8,128)S(1)} %copy-done.2), custom_call_target="tpu_custom_call" | custom-call | tf_op jit(solution)/shard_map/end/pallas_call | solution.py:73
  (3 shorter events, 0.0 us)
Async XLA Ops:
  2.5 22.0 %all-to-all-start = ((f32[8,32,128]{2,1,0:T(8,128)}), f32[8,32,128]{2,1,0:T(8,128)S(1)}, u32[]{:S(2)}, u32[]{:S(2)}) async-start(f32[8,32,128]{2,1,0:T(8,128)} %pack.1), calls=%async_computation | async-start | bytes 262144 | tf_op jit(solution)/shard_map/all_to_all | solution.py:332
  15.5 1.0 copy-start
  16.4 0.9 copy-start.1
  17.4 1.0 copy-start.3
  44.6 58.0 %copy-start.2 = (f32[2,8,8,512]{3,2,1,0:T(8,128)S(1)}, f32[2,8,8,512]{3,2,1,0:T(8,128)}, u32[]{:S(2)}) copy-start(f32[2,8,8,512]{3,2,1,0:T(8,128)} %duals_ref.3) | copy-start | bytes 786436
  96.6 6.0 %collective-permute-start = (f32[32,16,128]{2,1,0:T(8,128)S(1)}, f32[32,16,128]{2,1,0:T(8,128)S(1)}, u32[]{:S(2)}, u32[]{:S(2)}) collective-permute-start(f32[32,16,128]{2,1,0:T(8,128)S(1)} %slice.4), channel_id=1, source_target_pairs={{0,32},{32,0},{64,96},{96,64},{128,160},{160,128},{192,224},{224,1... | collective-permute-start | bytes 786440 | tf_op jit(solution)/shard_map/ppermute | solution.py:403

commit v3 on v2

--- a/solution.py
+++ b/solution.py
@@ -58,22 +58,23 @@
     return jnp.concatenate([high, low], axis=0)
 
 
-SMEM = pl.BlockSpec(memory_space=pltpu.SMEM)
 VMEM = pl.BlockSpec(memory_space=pltpu.VMEM)
-
-def call(kernel, outs, *args, scratch=(), fast=None, kinds=None, slow_outs=False, limit=12 << 20, name=None):
+HBM = pl.BlockSpec(memory_space=pltpu.HBM)
+
+
+def in_vmem(x):
+    return pltpu.with_memory_space_constraint(x, pltpu.MemorySpace.VMEM)
+
+
+def call(kernel, outs, *args, scratch=(), fast=None, kinds=None, limit=12 << 20, name=None):
     fast = range(len(args)) if fast is None else fast
-    args = [
-        pltpu.with_memory_space_constraint(a, pltpu.MemorySpace.VMEM) if n in fast else a
-        for n, a in enumerate(args)
-    ]
-    kind = jax.ShapeDtypeStruct if slow_outs else pltpu.VMEM
+    args = [in_vmem(a) if n in fast else a for n, a in enumerate(args)]
     many = isinstance(outs, list)
     kinds = kinds or [F32] * len(outs)
     return pl.pallas_call(
         kernel,
-        out_shape=tuple(kind(o, t) for o, t in zip(outs, kinds)) if many else kind(outs, F32),
-        in_specs=[SMEM if a.dtype == jnp.int32 and a.ndim == 1 else VMEM for a in args],
+        out_shape=tuple(pltpu.VMEM(o, t) for o, t in zip(outs, kinds)) if many else pltpu.VMEM(outs, F32),
+        in_specs=[VMEM for _ in args],
         out_specs=tuple(VMEM for _ in outs) if many else VMEM,
         scratch_shapes=list(scratch),
         compiler_params=pltpu.CompilerParams(vmem_limit_bytes=limit),
@@ -131,8 +132,13 @@
             out_ref[c * GROUPS + g, pl.ds(24, 8), :] = names
 
 
-def own_kernel(count, index_ref, gains_ref, duals_ref, poly_ref, out_ref):
-    freq, c, g = index_ref[0], index_ref[1], index_ref[2]
+def place_of():
+    own = lax.axis_index("r1") * 2 + lax.axis_index("r0")
+    return lax.axis_index("freq"), lax.axis_index("c"), lax.axis_index("g"), own
+
+
+def own_kernel(count, gains_ref, duals_ref, poly_ref, out_ref, cut_ref):
+    freq, c, g, own = place_of()
     basis = basis_of(freq * CHANS + c, count)
     sublane = lax.broadcasted_iota(jnp.int32, (DIRS, STATIONS), 0)
     for i in range(8):
@@ -142,8 +148,12 @@
         for n, tile in enumerate((gains_ref[c, i], duals_ref[c, i], prior)):
             for d in range(PAIR):
                 row = jnp.sum(jnp.where(sublane == d * GROUPS + g, tile, 0.0), axis=0, keepdims=True)
+                parts = [row[:, q * LANES : (q + 1) * LANES] for q in range(CUTS)]
+                chosen = parts[0]
                 for q in range(CUTS):
-                    out_ref[n, pl.ds(i * 8 + q * PAIR + d, 1), :] = row[:, q * LANES : (q + 1) * LANES]
+                    out_ref[n, pl.ds(i * 8 + q * PAIR + d, 1), :] = parts[q]
+                    chosen = jnp.where(own == q, parts[q], chosen)
+                cut_ref[n, pl.ds(d * 8 + i, 1), :] = chosen
 
 
 def looked_up(gains_ref, hot_ref, at_ref):
@@ -172,7 +182,7 @@
     return split([rows_ref[pl.ds(d * 8 + i, SOURCES, stride=32), :] for i in range(8)])
 
 
-def summed(rest, rows_ref, at_ref, hot_ref, out_ref, terms, total_ref):
+def summed(rest, rows_ref, at_ref, hot_ref, terms, total_ref):
     half = SOURCES * 24
     for d in range(PAIR):
         first, second = ends(at_ref, d)
@@ -191,11 +201,6 @@
     total = total[:24] + total[24:]
     for q in range(CUTS):
         total_ref[q] = total[:, q * LANES : (q + 1) * LANES]
-    for q in range(CUTS):
-        for d in range(PAIR):
-            part = total_ref[q, pl.ds(d * 12, 12), :]
-            for n in range(out_ref.shape[0]):
-                out_ref[n, pl.ds(q * PAIR + d, 12, stride=8), :] = part
 
 
 def model_of(rows_ref, at_ref):
@@ -216,24 +221,19 @@
             hot_ref[:, lanes] = jnp.where(station == name, 1.0, 0.0).astype(BF16)
     looked_up(own_ref.at[0], hot_ref, at)
     rest = split([rows_ref[pl.ds(16 + i, SOURCES, stride=32), :] for i in range(8)])
-    summed(rest, rows_ref, at, hot_ref, out_ref, terms, total)
+    summed(rest, rows_ref, at, hot_ref, terms, total)
+    for q in range(CUTS):
+        for d in range(PAIR):
+            part = total[q, pl.ds(d * 12, 12), :]
+            for n in range(out_ref.shape[0]):
+                out_ref[n, pl.ds(q * PAIR + d, 12, stride=8), :] = part
     model = model_of(rows_ref, at)
     for i in range(8):
         model_ref[pl.ds(i * 8, 8), :] = model[i]
 
 
-def stepped(arrived, gains_ref, own_ref, damping, put):
-    total = []
-    for i in range(12):
-        value = arrived[0, pl.ds(i * 8, 8), :]
-        for n in range(1, arrived.shape[0]):
-            value = value + arrived[n, pl.ds(i * 8, 8), :]
-        total.append(value)
-    tile = lambda ref, i: ref[pl.ds(i * 8, 8), :]
-    gains = [tile(gains_ref, i) for i in range(8)]
-    way = [
-        total[i] - tile(own_ref.at[1], i) - RHO * (gains[i] - tile(own_ref.at[2], i)) for i in range(8)
-    ]
+def stepped(total, gains, duals, prior, damping):
+    way = [total[i] - duals[i] - RHO * (gains[i] - prior[i]) for i in range(8)]
     top, bottom, cross_re, cross_im = total[8:]
     shift = damping * 0.5 * (top + bottom) + RHO
     upper = top + shift
@@ -245,14 +245,27 @@
         [zeros, -cross_im * scale, cross_im * scale, zeros],
     )
     step = flat(product(split(way), inverse))
-    new = [gains[i] + step[i] for i in range(8)]
-    for i in range(8):
-        put[pl.ds(i * 8, 8), :] = new[i]
-    return new
-
-
-def middle_kernel(damping, arrived, own_ref, rows_ref, hot_ref, model_ref, out_ref, gains_ref, at_ref):
-    stepped(arrived, own_ref.at[0], own_ref, damping, gains_ref)
+    return [gains[i] + step[i] for i in range(8)]
+
+
+def middle_kernel(
+    damping, arrived, own_ref, rows_ref, hot_ref, model_ref, out_ref, cut_ref, at_ref, gains_ref
+):
+    own = place_of()[3]
+    total = []
+    for i in range(12):
+        value = arrived[0, pl.ds(i * 8, 8), :]
+        for n in range(1, arrived.shape[0]):
+            value = value + arrived[n, pl.ds(i * 8, 8), :]
+        total.append(value)
+    start = [[own_ref[n, pl.ds(i * 8, 8), :] for i in range(8)] for n in range(3)]
+    new = stepped(total, *start, damping)
+    for i in range(8):
+        gains_ref[pl.ds(i * 8, 8), :] = new[i]
+        chosen = new[i][:PAIR]
+        for q in range(1, CUTS):
+            chosen = jnp.where(own == q, new[i][q * PAIR : (q + 1) * PAIR], chosen)
+        cut_ref[pl.ds(i, PAIR, stride=8), :] = chosen
     looked_up(gains_ref, hot_ref, at_ref)
     model = model_of(rows_ref, at_ref)
     for i in range(8):
@@ -261,31 +274,30 @@
             out_ref[n, pl.ds(i * 8, 8), :] = change
 
 
-def second_kernel(arrived, rows_ref, hot_ref, at_ref, out_ref, terms, total):
+def second_kernel(arrived, rows_ref, hot_ref, at_ref, out_ref, terms):
     rest = []
     for i in range(8):
         value = rows_ref[pl.ds(16 + i, SOURCES, stride=32), :]
         for n in range(arrived.shape[0]):
             value = value + arrived[n, pl.ds(i * 8, 8), :]
         rest.append(value)
-    summed(split(rest), rows_ref, at_ref, hot_ref, out_ref, terms, total)
-
-
-def last_kernel(damping, count, gram, index_ref, arrived, gains_ref, own_ref, fit_ref, mine_ref, new):
-    gains = stepped(arrived, gains_ref, own_ref, damping, new)
-    freq, c, q = index_ref[0], index_ref[1], index_ref[3]
+    summed(split(rest), rows_ref, at_ref, hot_ref, terms, out_ref)
+
+
+def last_kernel(damping, count, gram, arrived, gains_ref, own_ref, fit_ref, mine_ref, total_ref):
+    value = arrived[0]
+    for n in range(1, arrived.shape[0]):
+        value = value + arrived[n]
+    total_ref[...] = value
+    total = [total_ref[pl.ds(i, PAIR, stride=12), :] for i in range(12)]
+    gains = [gains_ref[pl.ds(i, PAIR, stride=8), :] for i in range(8)]
+    duals, prior = [[own_ref[n, pl.ds(i, PAIR, stride=8), :] for i in range(8)] for n in (1, 2)]
+    new = stepped(total, gains, duals, prior, damping)
+    for i in range(8):
+        mine_ref[pl.ds(i, PAIR, stride=8), :] = new[i]
+    freq, c, _, _ = place_of()
     weights = weights_of(basis_of(freq * CHANS + c, count), gram)
-
-    def own_cut(tile):
-        chosen = tile[:PAIR]
-        for n in range(1, CUTS):
-            chosen = jnp.where(q == n, tile[n * PAIR : (n + 1) * PAIR], chosen)
-        return chosen
-
-    mine_ref[...] = jnp.concatenate([own_cut(g) for g in gains], axis=0)
-    mixed = jnp.concatenate(
-        [own_cut(gains[i] + own_ref[1, pl.ds(i * 8, 8), :] / RHO) for i in range(8)], axis=0
-    )
+    mixed = mine_ref[...] + own_ref[1] / RHO
     for n in range(fit_ref.shape[0]):
         fit_ref[n] = weights[n % POLY] * mixed
 
@@ -300,32 +312,57 @@
         out_ref[n, pl.ds(16, 16), :] = total
 
 
-def end_kernel(count, index_ref, all_ref, other_ref, duals_ref, gains_out, duals_out, poly_out):
-    freq = index_ref[0]
+def tile_of(ref, c, q, row, size):
+    place = c * 16 + (q // 2) * 8 + q % 2
+    return jnp.concatenate(
+        [ref[pl.ds(place * size + row + d * 8, GROUPS, stride=2 * size), :] for d in range(PAIR)], axis=0
+    )
+
+
+def near_kernel(count, all_ref, duals_ref, gains_out, poly_out, part_ref, gains, poly, sems):
+    freq = lax.axis_index("freq")
     core = freq % 2
     basis = [basis_of(freq * CHANS + c, count) for c in range(CHANS)]
     mine = [[jnp.where(core == 0, basis[c][j], basis[c][j + 2]) for j in range(2)] for c in range(CHANS)]
+    to_gains = pltpu.make_async_copy(gains, gains_out, sems.at[0])
+    to_poly = pltpu.make_async_copy(poly, poly_out.at[pl.ds(2 * core, 2)], sems.at[1])
+    for i in range(8):
+        for q in range(CUTS):
+            for c in range(CHANS):
+                gains[c, i, :, q * LANES : (q + 1) * LANES] = tile_of(all_ref, c, q, i, 32)
+    to_gains.start()
+    for i in range(8):
+        for q in range(CUTS):
+            for j in range(2):
+                poly[j, i, :, q * LANES : (q + 1) * LANES] = tile_of(all_ref, j, q, 16 + i, 32)
+    to_poly.start()
+    for c in range(CHANS):
+        for i in range(8):
+            prior = mine[c][0] * poly[0, i] + mine[c][1] * poly[1, i]
+            part_ref[c, i] = duals_ref[c, i] + RHO * (gains[c, i] - prior)
+    to_gains.wait()
+    to_poly.wait()
+
+
+def far_kernel(count, other_ref, part_ref, half_ref, duals_out, poly_out, duals, poly, sems):
+    del half_ref
+    freq = lax.axis_index("freq")
+    core = freq % 2
+    basis = [basis_of(freq * CHANS + c, count) for c in range(CHANS)]
     his = [[jnp.where(core == 0, basis[c][j + 2], basis[c][j]) for j in range(2)] for c in range(CHANS)]
-
-    def tile(ref, c, q, row, size):
-        place = c * 16 + (q // 2) * 8 + q % 2
-        return jnp.concatenate(
-            [ref[pl.ds(place * size + row + d, GROUPS, stride=2 * size), :] for d in range(PAIR)], axis=0
-        )
-
+    to_duals = pltpu.make_async_copy(duals, duals_out, sems.at[0])
+    to_poly = pltpu.make_async_copy(poly, poly_out.at[pl.ds(2 - 2 * core, 2)], sems.at[1])
     for i in range(8):
         for q in range(CUTS):
-            lanes = pl.ds(q * LANES, LANES)
-            own = [tile(all_ref, c, q, 16 + i * PAIR, 32) for c in range(CHANS)]
-            far = [tile(other_ref, c, q, i * PAIR, 16) for c in range(CHANS)]
             for j in range(2):
-                poly_out[2 * core + j, i, :, lanes] = own[j]
-                poly_out[2 - 2 * core + j, i, :, lanes] = far[j]
-            for c in range(CHANS):
-                gains = tile(all_ref, c, q, i * PAIR, 32)
-                gains_out[c, i, :, lanes] = gains
-                prior = mine[c][0] * own[0] + mine[c][1] * own[1] + his[c][0] * far[0] + his[c][1] * far[1]
-                duals_out[c, i, :, lanes] = duals_ref[c, i, :, lanes] + RHO * (gains - prior)
+                poly[j, i, :, q * LANES : (q + 1) * LANES] = tile_of(other_ref, j, q, i, 16)
+    to_poly.start()
+    for c in range(CHANS):
+        for i in range(8):
+            duals[c, i] = part_ref[c, i] - RHO * (his[c][0] * poly[0, i] + his[c][1] * poly[1, i])
+    to_duals.start()
+    to_poly.wait()
+    to_duals.wait()
 
 
 def exchanged(x, axis):
@@ -339,13 +376,11 @@
     freqs = lax.axis_size("freq")
     times = lax.axis_size(TIMES)
     count = CHANS * freqs
-    index = jnp.stack(
-        [lax.axis_index("freq"), lax.axis_index("c"), lax.axis_index("g"), lax.axis_index(("r1", "r0"))]
-    ).astype(jnp.int32)
     sums_shape = (CUTS, 12 * 8, LANES)
     tiles = (64, LANES)
     share = (16, LANES)
-    work = [pltpu.VMEM((2 * SOURCES * 24, ROWS), F32), pltpu.VMEM((CUTS, 24, LANES), F32)]
+    work = pltpu.VMEM((2 * SOURCES * 24, ROWS), F32)
+    quarters = (CUTS, 24, LANES)
 
     sent = call(
         pack_kernel,
@@ -359,8 +394,15 @@
         scratch=[pltpu.VMEM((CHANS, 64, ROWS), F32)],
         name="pack",
     )
-    own = call(
-        functools.partial(own_kernel, count), (3, *tiles), index, gains_start, duals_start, poly_start, fast=[], name="own"
+    own, cut = call(
+        functools.partial(own_kernel, count),
+        [(3, *tiles), (3, *share)],
+        gains_start,
+        duals_start,
+        poly_start,
+        fast=[],
+        limit=60 << 20,
+        name="own",
     )
     rows = exchanged(sent, ("c", "g")).reshape(SOURCES * 32, ROWS)
     sums, hot, model = call(
@@ -369,32 +411,31 @@
         rows,
         own,
         kinds=[F32, BF16, F32],
-        scratch=[pltpu.VMEM((2 * SOURCES * 16, ROWS), F32), *work],
+        scratch=[pltpu.VMEM((2 * SOURCES * 16, ROWS), F32), work, pltpu.VMEM(quarters, F32)],
         name="start",
     )
     sums = exchanged(sums, ("r1", "r0"))
     change, gains, at = call(
         functools.partial(middle_kernel, 12.0),
-        [(GROUPS, *tiles), tiles, (2 * SOURCES * 16, ROWS)],
+        [(GROUPS, *tiles), share, (2 * SOURCES * 16, ROWS)],
         sums,
         own,
         rows,
         hot,
         model,
+        scratch=[pltpu.VMEM(tiles, F32)],
         name="middle",
     )
     change = exchanged(change, "g")
-    sums = call(second_kernel, sums_shape, change, rows, hot, at, scratch=work, name="second")
+    sums = call(second_kernel, quarters, change, rows, hot, at, scratch=[work], name="second")
     sums = exchanged(sums, ("r1", "r0"))
     fits, mine = call(
         functools.partial(last_kernel, 6.0, count, inverse_gram(count)),
         [(freqs * CHANS, *share), share],
-        index,
         sums,
         gains,
-        own,
-        fast=[1, 2, 3],
-        scratch=[pltpu.VMEM(tiles, F32)],
+        cut,
+        scratch=[pltpu.VMEM((24, LANES), F32)],
         name="last",
     )
     fits = exchanged(fits, ("freq", "c"))
@@ -402,17 +443,30 @@
     everything = exchanged(copies, TIMES)
     other = lax.ppermute(everything[:, 16:], "freq", [(i, i ^ 1) for i in range(freqs)])
     block = (CHANS, 8, DIRS, STATIONS)
-    return call(
-        functools.partial(end_kernel, count),
-        [block, block, (POLY, 8, DIRS, STATIONS)],
-        index,
-        everything.reshape(times * 32, LANES),
-        other.reshape(times * 16, LANES),
-        duals_start,
-        fast=[1, 2, 3],
-        slow_outs=True,
-        name="end",
-    )
+    held = [pltpu.VMEM(block, F32), pltpu.VMEM(block, F32), pltpu.SemaphoreType.DMA((2,))]
+    full = (POLY, 8, DIRS, STATIONS)
+    everything = in_vmem(everything.reshape(times * 32, LANES))
+    gains, half, part = pl.pallas_call(
+        functools.partial(near_kernel, count),
+        out_shape=(pltpu.HBM(block, F32), pltpu.HBM(full, F32), pltpu.VMEM(block, F32)),
+        in_specs=[VMEM, VMEM],
+        out_specs=(HBM, HBM, VMEM),
+        scratch_shapes=held,
+        compiler_params=pltpu.CompilerParams(vmem_limit_bytes=12 << 20),
+        cost_estimate=pl.CostEstimate(flops=1000000, bytes_accessed=2000000, transcendentals=0),
+        name="near",
+    )(everything, in_vmem(duals_start))
+    duals, polynomial = pl.pallas_call(
+        functools.partial(far_kernel, count),
+        out_shape=(pltpu.HBM(block, F32), pltpu.HBM(full, F32)),
+        in_specs=[VMEM, VMEM, HBM],
+        out_specs=(HBM, HBM),
+        input_output_aliases={2: 1},
+        scratch_shapes=held,
+        compiler_params=pltpu.CompilerParams(vmem_limit_bytes=12 << 20),
+        name="far",
+    )(in_vmem(other.reshape(times * 16, LANES)), part, half)
+    return (gains, duals, polynomial)
 
 
 def solution(mesh):

time: 105 us -> 103 us (0.981)
  local copies, waits for them, and re-layouts: 2.97 us -> 0.02 us
  waiting for transfers between devices: 6.53 us -> 7.79 us
    unnamed x8 -> x2, local copies, waits for them, and re-layouts: 2.95 us -> 0.01 us
    all_to_all x1, waiting for transfers between devices: 5.39 us -> 7.73 us  [exchanged(): return lax.all_to_all(x, axis, split_axis=0, concat_axis=0, tiled=True)]
    ppermute x1, waiting for transfers between devices: 1.14 us -> 0.06 us  [shards(): lax.ppermute(everything[:, 16:], 'freq', [(i, i ^ 1) for i in range(freqs)])]
    pallas_call x8 -> x9, Pallas kernels: 8.36 us -> 8.52 us  [the longest x7 6.48 us: call(): pl.pallas_call(kernel, out_shape=tuple((pltpu.VMEM(o, t) for o, t in zip(...]
  transfers between devices with their start and end apart: 2 -> 2, of which waited for: 2 -> 2; matrix products, arithmetic and copies ran while one was open for 0% -> 0% of each run, Pallas kernels for 1% -> 2%
where the time goes in v3:
time: 103 us; the launch traced here: 102 us
  blocking collectives  67.5 us (66%)
  starting transfers between devices  17.7 us (17%)
  Pallas kernels  8.52 us (8%)
  waiting for transfers between devices  7.79 us (8%)
    all_to_all x5, blocking collectives, exchanged(): return lax.all_to_all(x, axis, split_axis=0, concat_axis=0, tiled=True)  67.5 us
    all_to_all x1, starting transfers between devices, exchanged(): return lax.all_to_all(x, axis, split_axis=0, concat_axis=0, tiled=True)  12.9 us
    all_to_all x1, waiting for transfers between devices, exchanged(): return lax.all_to_all(x, axis, split_axis=0, concat_axis=0, tiled=True)  7.73 us
    pallas_call x7, Pallas kernels, call(): pl.pallas_call(kernel, out_shape=tuple((pltpu.VMEM(o, t) for o, t in zip(...  6.48 us
    ppermute x1, starting transfers between devices, shards(): lax.ppermute(everything[:, 16:], 'freq', [(i, i ^ 1) for i in range(freqs)])  4.81 us
  transfers between devices with their start and end apart: 2, of which 2 were waited for; matrix products, arithmetic and copies ran while one was open for 0% of the time, Pallas kernels for 2%

profile of v3, /device:TPU:1, one launch (start us, length us, event | category | flops | bytes accessed | tf_op | source)
XLA Modules:
  0.0 102.2 jit_solution(13567830275204519130)
XLA Ops:
  0.6 1.9 %pack.1 = f32[8,32,128]{2,1,0:T(8,128)} custom-call(f32[2,8,8,512]{3,2,1,0:T(8,128)} %gains_ref.3, bf16[2,8,8,128]{3,2,1,0:T(8,128)(2,1)} %coh_ref.1, f32[2,8,128]{2,1,0:T(8,128)} %vis_ref.1, s32[2,128]{1,0:T(2,128)} %pairs_ref.1), custom_call_target="tpu_custom_call" | custom-call | tf_op jit(solution)/shard_map/pack/pallas_call | solution.py:74
  2.5 12.9 %all-to-all-start = ((f32[8,32,128]{2,1,0:T(8,128)}), f32[8,32,128]{2,1,0:T(8,128)S(1)}, u32[]{:S(2)}, u32[]{:S(2)}) async-start(f32[8,32,128]{2,1,0:T(8,128)} %pack.1), calls=%async_computation | async-start | bytes 262144 | tf_op jit(solution)/shard_map/all_to_all | solution.py:369
  15.4 1.4 %own.1 = (f32[3,64,128]{2,1,0:T(8,128)S(1)}, f32[3,16,128]{2,1,0:T(8,128)S(1)}) custom-call(f32[2,8,8,512]{3,2,1,0:T(8,128)} %gains_ref.3, f32[2,8,8,512]{3,2,1,0:T(8,128)} %duals_ref.3, f32[4,8,8,512]{3,2,1,0:T(8,128)} %poly_ref.1), custom_call_target="tpu_custom_call" | custom-call | tf_op jit(solution)/shard_map/own/pallas_call | solution.py:74
  16.8 7.7 %all-to-all-done = f32[8,32,128]{2,1,0:T(8,128)S(1)} async-done(((f32[8,32,128]{2,1,0:T(8,128)}), f32[8,32,128]{2,1,0:T(8,128)S(1)}, u32[]{:S(2)}, u32[]{:S(2)}) %all-to-all-start) | async-done | bytes 131104 | tf_op jit(solution)/shard_map/all_to_all | solution.py:369
  24.6 1.7 %start.1 = (f32[4,96,128]{2,1,0:T(8,128)S(1)}, bf16[512,2048]{1,0:T(8,128)(2,1)S(1)}, f32[64,128]{1,0:T(8,128)S(1)}) custom-call(f32[256,128]{1,0:T(8,128)S(1)} %bitcast.4, f32[3,64,128]{2,1,0:T(8,128)S(1)} %get-tuple-element.18.own_ref), custom_call_target="tpu_custom_call" | custom-call | tf_op jit(solution)/shard_map/start/pallas_call | solution.py:74
  26.3 7.4 %all_to_all.30.arrived = f32[4,96,128]{2,1,0:T(8,128)S(1)} all-to-all(f32[4,96,128]{2,1,0:T(8,128)S(1)} %get-tuple-element.19), channel_id=1, replica_groups=mesh['freq'=16,'c'=2,'r1'=2,'g'=4,'r0'=2] {'r1','r0'}, dimensions={0} | all-to-all | bytes 393216 | tf_op jit(solution)/shard_map/all_to_all | solution.py:369
  33.7 0.5 middle.1
  34.2 9.6 %all_to_all.31.arrived = f32[4,64,128]{2,1,0:T(8,128)S(1)} all-to-all(f32[4,64,128]{2,1,0:T(8,128)S(1)} %get-tuple-element.22), channel_id=1, replica_groups=mesh['freq'=16,'c'=2,'r1'=2,'g'=4,'r0'=2] {'g'}, dimensions={0} | all-to-all | bytes 262144 | tf_op jit(solution)/shard_map/all_to_all | solution.py:369
  43.8 0.8 second.1
  44.6 0.0 copy-start
  44.6 6.1 %all_to_all.32.arrived = f32[4,24,128]{2,1,0:T(8,128)S(1)} all-to-all(f32[4,24,128]{2,1,0:T(8,128)S(1)} %second.1), channel_id=1, replica_groups=mesh['freq'=16,'c'=2,'r1'=2,'g'=4,'r0'=2] {'r1','r0'}, dimensions={0} | all-to-all | bytes 98304 | tf_op jit(solution)/shard_map/all_to_all | solution.py:369
  50.8 0.1 last.1
  50.8 25.4 %all_to_all.33.arrived = f32[32,16,128]{2,1,0:T(8,128)S(1)} all-to-all(f32[32,16,128]{2,1,0:T(8,128)S(1)} %get-tuple-element.26), channel_id=1, replica_groups=mesh['freq'=16,'c'=2,'r1'=2,'g'=4,'r0'=2] {'freq','c'}, dimensions={0} | all-to-all | bytes 524288 | tf_op jit(solution)/shard_map/all_to_all | solution.py:369
  76.3 0.1 joined.1
  76.3 18.9 %all_to_all.34 = f32[32,32,128]{2,1,0:T(8,128)S(1)} all-to-all(f32[32,32,128]{2,1,0:T(8,128)S(1)} %joined.1), channel_id=1, replica_groups=mesh['freq'=16,'c'=2,'r1'=2,'g'=4,'r0'=2] {'c','r1','g','r0'}, dimensions={0} | all-to-all | bytes 1048576 | tf_op jit(solution)/shard_map/all_to_all | solution.py:369
  95.3 4.8 %collective-permute-start = (f32[32,16,128]{2,1,0:T(8,128)S(1)}, f32[32,16,128]{2,1,0:T(8,128)S(1)}, u32[]{:S(2)}, u32[]{:S(2)}) collective-permute-start(f32[32,16,128]{2,1,0:T(8,128)S(1)} %slice.4), channel_id=1, source_target_pairs={{0,32},{32,0},{64,96},{96,64},{128,160},{160,128},{192,224},{224,1... | collective-permute-start | bytes 786440 | tf_op jit(solution)/shard_map/ppermute | solution.py:444
  100.1 0.0 copy-done
  100.1 1.1 %near.1 = (f32[2,8,8,512]{3,2,1,0:T(8,128)}, f32[4,8,8,512]{3,2,1,0:T(8,128)}, f32[2,8,8,512]{3,2,1,0:T(8,128)S(1)}) custom-call(f32[1024,128]{1,0:T(8,128)S(1)} %bitcast.3, f32[2,8,8,512]{3,2,1,0:T(8,128)S(1)} %copy-done), custom_call_target="tpu_custom_call" | custom-call | flops 1000000 | bytes 2000000 | tf_op jit(solution)/shard_map/near/pallas_call | solution.py:449
  101.2 0.1 collective-permute-done
  101.3 1.0 far.1
  (1 shorter events, 0.0 us)
Async XLA Ops:
  2.5 22.0 %all-to-all-start = ((f32[8,32,128]{2,1,0:T(8,128)}), f32[8,32,128]{2,1,0:T(8,128)S(1)}, u32[]{:S(2)}, u32[]{:S(2)}) async-start(f32[8,32,128]{2,1,0:T(8,128)} %pack.1), calls=%async_computation | async-start | bytes 262144 | tf_op jit(solution)/shard_map/all_to_all | solution.py:369
  44.6 55.5 %copy-start = (f32[2,8,8,512]{3,2,1,0:T(8,128)S(1)}, f32[2,8,8,512]{3,2,1,0:T(8,128)}, u32[]{:S(2)}) copy-start(f32[2,8,8,512]{3,2,1,0:T(8,128)} %duals_ref.3) | copy-start | bytes 786436
  95.3 6.0 %collective-permute-start = (f32[32,16,128]{2,1,0:T(8,128)S(1)}, f32[32,16,128]{2,1,0:T(8,128)S(1)}, u32[]{:S(2)}, u32[]{:S(2)}) collective-permute-start(f32[32,16,128]{2,1,0:T(8,128)S(1)} %slice.4), channel_id=1, source_target_pairs={{0,32},{32,0},{64,96},{96,64},{128,160},{160,128},{192,224},{224,1... | collective-permute-start | bytes 786440 | tf_op jit(solution)/shard_map/ppermute | solution.py:444

commit v4 on v3

--- a/solution.py
+++ b/solution.py
@@ -87,14 +87,10 @@
     return [1.0 + 0.0 * x, x, 1.5 * x * x - 0.5, 2.5 * x * x * x - 1.5 * x]
 
 
-def inverse_gram(count):
+def fit_weights(count):
     x = (2.0 * np.arange(count) + 1.0) / count - 1.0
     basis = np.stack([np.ones_like(x), x, 1.5 * x * x - 0.5, 2.5 * x**3 - 1.5 * x], axis=1)
-    return np.linalg.inv(basis.T @ basis)
-
-
-def weights_of(basis, gram):
-    return [sum(float(gram[j, i]) * basis[i] for i in range(POLY)) for j in range(POLY)]
+    return np.linalg.solve(basis.T @ basis, basis.T)
 
 
 def split(parts):
@@ -284,7 +280,7 @@
     summed(split(rest), rows_ref, at_ref, hot_ref, terms, out_ref)
 
 
-def last_kernel(damping, count, gram, arrived, gains_ref, own_ref, fit_ref, mine_ref, total_ref):
+def last_kernel(damping, arrived, gains_ref, own_ref, out_ref, total_ref, new_ref):
     value = arrived[0]
     for n in range(1, arrived.shape[0]):
         value = value + arrived[n]
@@ -294,68 +290,73 @@
     duals, prior = [[own_ref[n, pl.ds(i, PAIR, stride=8), :] for i in range(8)] for n in (1, 2)]
     new = stepped(total, gains, duals, prior, damping)
     for i in range(8):
-        mine_ref[pl.ds(i, PAIR, stride=8), :] = new[i]
-    freq, c, _, _ = place_of()
-    weights = weights_of(basis_of(freq * CHANS + c, count), gram)
-    mixed = mine_ref[...] + own_ref[1] / RHO
-    for n in range(fit_ref.shape[0]):
-        fit_ref[n] = weights[n % POLY] * mixed
-
-
-def joined_kernel(arrived, gains_ref, out_ref):
-    total = arrived[0]
-    for n in range(1, arrived.shape[0]):
-        total = total + arrived[n]
-    gains = gains_ref[...]
+        new_ref[pl.ds(i, PAIR, stride=8), :] = new[i]
+    mixed = new_ref[...] + own_ref[1] / RHO
     for n in range(out_ref.shape[0]):
-        out_ref[n, pl.ds(0, 16), :] = gains
-        out_ref[n, pl.ds(16, 16), :] = total
-
-
-def tile_of(ref, c, q, row, size):
-    place = c * 16 + (q // 2) * 8 + q % 2
+        out_ref[n] = mixed
+
+
+def joined_kernel(weights, arrived, out_ref):
+    freq = lax.axis_index("freq")
+    first = freq % 2 == 0
+    parts = [arrived[freq * CHANS + c] for c in range(CHANS)]
+    mixed = [arrived[n] for n in range(arrived.shape[0])]
+    for j in range(2):
+        total = None
+        for n, value in enumerate(mixed):
+            weight = jnp.where(first, float(weights[j, n]), float(weights[j + 2, n]))
+            total = weight * value if total is None else total + weight * value
+        parts.append(total)
+    for n in range(out_ref.shape[0]):
+        for k, part in enumerate(parts):
+            out_ref[n, pl.ds(k * 16, 16), :] = part
+
+
+def tile_of(ref, q, row, size):
+    place = (q // 2) * 8 + q % 2
     return jnp.concatenate(
         [ref[pl.ds(place * size + row + d * 8, GROUPS, stride=2 * size), :] for d in range(PAIR)], axis=0
     )
 
 
-def near_kernel(count, all_ref, duals_ref, gains_out, poly_out, part_ref, gains, poly, sems):
+def sides(count):
     freq = lax.axis_index("freq")
     core = freq % 2
     basis = [basis_of(freq * CHANS + c, count) for c in range(CHANS)]
-    mine = [[jnp.where(core == 0, basis[c][j], basis[c][j + 2]) for j in range(2)] for c in range(CHANS)]
+    mine = [[jnp.where(core == 0, b[j], b[j + 2]) for j in range(2)] for b in basis]
+    his = [[jnp.where(core == 0, b[j + 2], b[j]) for j in range(2)] for b in basis]
+    return core, mine, his
+
+
+def near_kernel(count, all_ref, duals_ref, gains_out, poly_out, part_ref, gains, poly, sems):
+    core, mine, _ = sides(count)
     to_gains = pltpu.make_async_copy(gains, gains_out, sems.at[0])
     to_poly = pltpu.make_async_copy(poly, poly_out.at[pl.ds(2 * core, 2)], sems.at[1])
     for i in range(8):
         for q in range(CUTS):
-            for c in range(CHANS):
-                gains[c, i, :, q * LANES : (q + 1) * LANES] = tile_of(all_ref, c, q, i, 32)
-    to_gains.start()
-    for i in range(8):
-        for q in range(CUTS):
+            lanes = slice(q * LANES, (q + 1) * LANES)
             for j in range(2):
-                poly[j, i, :, q * LANES : (q + 1) * LANES] = tile_of(all_ref, j, q, 16 + i, 32)
+                poly[j, i, :, lanes] = tile_of(all_ref, q, 32 + j * 16 + i, 64)
     to_poly.start()
     for c in range(CHANS):
         for i in range(8):
-            prior = mine[c][0] * poly[0, i] + mine[c][1] * poly[1, i]
-            part_ref[c, i] = duals_ref[c, i] + RHO * (gains[c, i] - prior)
+            mixed = jnp.concatenate([tile_of(all_ref, q, c * 16 + i, 64) for q in range(CUTS)], axis=1)
+            gains[c, i] = mixed - duals_ref[c, i] / RHO
+            part_ref[c, i] = RHO * (mixed - (mine[c][0] * poly[0, i] + mine[c][1] * poly[1, i]))
+    to_gains.start()
+    to_poly.wait()
     to_gains.wait()
-    to_poly.wait()
 
 
 def far_kernel(count, other_ref, part_ref, half_ref, duals_out, poly_out, duals, poly, sems):
     del half_ref
-    freq = lax.axis_index("freq")
-    core = freq % 2
-    basis = [basis_of(freq * CHANS + c, count) for c in range(CHANS)]
-    his = [[jnp.where(core == 0, basis[c][j + 2], basis[c][j]) for j in range(2)] for c in range(CHANS)]
+    core, _, his = sides(count)
     to_duals = pltpu.make_async_copy(duals, duals_out, sems.at[0])
     to_poly = pltpu.make_async_copy(poly, poly_out.at[pl.ds(2 - 2 * core, 2)], sems.at[1])
     for i in range(8):
         for q in range(CUTS):
             for j in range(2):
-                poly[j, i, :, q * LANES : (q + 1) * LANES] = tile_of(other_ref, j, q, i, 16)
+                poly[j, i, :, q * LANES : (q + 1) * LANES] = tile_of(other_ref, q, j * 16 + i, 32)
     to_poly.start()
     for c in range(CHANS):
         for i in range(8):
@@ -429,23 +430,24 @@
     change = exchanged(change, "g")
     sums = call(second_kernel, quarters, change, rows, hot, at, scratch=[work], name="second")
     sums = exchanged(sums, ("r1", "r0"))
-    fits, mine = call(
-        functools.partial(last_kernel, 6.0, count, inverse_gram(count)),
-        [(freqs * CHANS, *share), share],
+    mixed = call(
+        functools.partial(last_kernel, 6.0),
+        (freqs * CHANS, *share),
         sums,
         gains,
         cut,
-        scratch=[pltpu.VMEM((24, LANES), F32)],
+        scratch=[pltpu.VMEM((24, LANES), F32), pltpu.VMEM(share, F32)],
         name="last",
     )
-    fits = exchanged(fits, ("freq", "c"))
-    copies = call(joined_kernel, (times, 32, LANES), fits, mine, name="joined")
-    everything = exchanged(copies, TIMES)
-    other = lax.ppermute(everything[:, 16:], "freq", [(i, i ^ 1) for i in range(freqs)])
+    mixed = exchanged(mixed, ("freq", "c"))
+    members = times // CHANS
+    copies = call(functools.partial(joined_kernel, fit_weights(count)), (members, 64, LANES), mixed, name="joined")
+    everything = exchanged(copies, ("r1", "g", "r0"))
+    other = lax.ppermute(everything[:, 32:], "freq", [(i, i ^ 1) for i in range(freqs)])
     block = (CHANS, 8, DIRS, STATIONS)
     held = [pltpu.VMEM(block, F32), pltpu.VMEM(block, F32), pltpu.SemaphoreType.DMA((2,))]
     full = (POLY, 8, DIRS, STATIONS)
-    everything = in_vmem(everything.reshape(times * 32, LANES))
+    everything = in_vmem(everything.reshape(members * 64, LANES))
     gains, half, part = pl.pallas_call(
         functools.partial(near_kernel, count),
         out_shape=(pltpu.HBM(block, F32), pltpu.HBM(full, F32), pltpu.VMEM(block, F32)),
@@ -465,7 +467,7 @@
         scratch_shapes=held,
         compiler_params=pltpu.CompilerParams(vmem_limit_bytes=12 << 20),
         name="far",
-    )(in_vmem(other.reshape(times * 16, LANES)), part, half)
+    )(in_vmem(other.reshape(members * 32, LANES)), part, half)
     return (gains, duals, polynomial)
 
 

time: 103 us -> 99.5 us (0.966)
  blocking collectives: 67.5 us -> 63.4 us
    all_to_all x5, blocking collectives: 67.5 us -> 63.4 us  [exchanged(): return lax.all_to_all(x, axis, split_axis=0, concat_axis=0, tiled=True)]
  transfers between devices with their start and end apart: 2 -> 2, of which waited for: 2 -> 1; matrix products, arithmetic and copies ran while one was open for 0% -> 0% of each run, Pallas kernels for 2% -> 3%
where the time goes in v4:
time: 99.5 us; the launch traced here: 98.3 us
  blocking collectives  63.4 us (64%)
  starting transfers between devices  17.9 us (18%)
  Pallas kernels  8.54 us (9%)
  waiting for transfers between devices  7.78 us (8%)
    all_to_all x5, blocking collectives, exchanged(): return lax.all_to_all(x, axis, split_axis=0, concat_axis=0, tiled=True)  63.4 us
    all_to_all x1, starting transfers between devices, exchanged(): return lax.all_to_all(x, axis, split_axis=0, concat_axis=0, tiled=True)  12.9 us
    all_to_all x1, waiting for transfers between devices, exchanged(): return lax.all_to_all(x, axis, split_axis=0, concat_axis=0, tiled=True)  7.73 us
    pallas_call x7, Pallas kernels, call(): pl.pallas_call(kernel, out_shape=tuple((pltpu.VMEM(o, t) for o, t in zip(...  6.49 us
    ppermute x1, starting transfers between devices, shards(): lax.ppermute(everything[:, 32:], 'freq', [(i, i ^ 1) for i in range(freqs)])  5 us
  transfers between devices with their start and end apart: 2, of which 1 were waited for; matrix products, arithmetic and copies ran while one was open for 0% of the time, Pallas kernels for 3%

profile of v4, /device:TPU:1, one launch (start us, length us, event | category | flops | bytes accessed | tf_op | source)
XLA Modules:
  0.0 98.3 jit_solution(14435998558284671243)
XLA Ops:
  0.6 1.9 %pack.1 = f32[8,32,128]{2,1,0:T(8,128)} custom-call(f32[2,8,8,512]{3,2,1,0:T(8,128)} %gains_ref.3, bf16[2,8,8,128]{3,2,1,0:T(8,128)(2,1)} %coh_ref.1, f32[2,8,128]{2,1,0:T(8,128)} %vis_ref.1, s32[2,128]{1,0:T(2,128)} %pairs_ref.1), custom_call_target="tpu_custom_call" | custom-call | tf_op jit(solution)/shard_map/pack/pallas_call | solution.py:74
  2.5 12.9 %all-to-all-start = ((f32[8,32,128]{2,1,0:T(8,128)}), f32[8,32,128]{2,1,0:T(8,128)S(1)}, u32[]{:S(2)}, u32[]{:S(2)}) async-start(f32[8,32,128]{2,1,0:T(8,128)} %pack.1), calls=%async_computation | async-start | bytes 262144 | tf_op jit(solution)/shard_map/all_to_all | solution.py:370
  15.4 1.4 %own.1 = (f32[3,64,128]{2,1,0:T(8,128)S(1)}, f32[3,16,128]{2,1,0:T(8,128)S(1)}) custom-call(f32[2,8,8,512]{3,2,1,0:T(8,128)} %gains_ref.3, f32[2,8,8,512]{3,2,1,0:T(8,128)} %duals_ref.3, f32[4,8,8,512]{3,2,1,0:T(8,128)} %poly_ref.1), custom_call_target="tpu_custom_call" | custom-call | tf_op jit(solution)/shard_map/own/pallas_call | solution.py:74
  16.8 7.7 %all-to-all-done = f32[8,32,128]{2,1,0:T(8,128)S(1)} async-done(((f32[8,32,128]{2,1,0:T(8,128)}), f32[8,32,128]{2,1,0:T(8,128)S(1)}, u32[]{:S(2)}, u32[]{:S(2)}) %all-to-all-start) | async-done | bytes 131104 | tf_op jit(solution)/shard_map/all_to_all | solution.py:370
  24.6 1.7 %start.1 = (f32[4,96,128]{2,1,0:T(8,128)S(1)}, bf16[512,2048]{1,0:T(8,128)(2,1)S(1)}, f32[64,128]{1,0:T(8,128)S(1)}) custom-call(f32[256,128]{1,0:T(8,128)S(1)} %bitcast.4, f32[3,64,128]{2,1,0:T(8,128)S(1)} %get-tuple-element.16.own_ref), custom_call_target="tpu_custom_call" | custom-call | tf_op jit(solution)/shard_map/start/pallas_call | solution.py:74
  26.3 7.4 %all_to_all.30.arrived = f32[4,96,128]{2,1,0:T(8,128)S(1)} all-to-all(f32[4,96,128]{2,1,0:T(8,128)S(1)} %get-tuple-element.17), channel_id=1, replica_groups=mesh['freq'=16,'c'=2,'r1'=2,'g'=4,'r0'=2] {'r1','r0'}, dimensions={0} | all-to-all | bytes 393216 | tf_op jit(solution)/shard_map/all_to_all | solution.py:370
  33.7 0.5 middle.1
  34.2 9.6 %all_to_all.31.arrived = f32[4,64,128]{2,1,0:T(8,128)S(1)} all-to-all(f32[4,64,128]{2,1,0:T(8,128)S(1)} %get-tuple-element.20), channel_id=1, replica_groups=mesh['freq'=16,'c'=2,'r1'=2,'g'=4,'r0'=2] {'g'}, dimensions={0} | all-to-all | bytes 262144 | tf_op jit(solution)/shard_map/all_to_all | solution.py:370
  43.8 0.8 second.1
  44.6 0.0 copy-start
  44.6 6.1 %all_to_all.32.arrived = f32[4,24,128]{2,1,0:T(8,128)S(1)} all-to-all(f32[4,24,128]{2,1,0:T(8,128)S(1)} %second.1), channel_id=1, replica_groups=mesh['freq'=16,'c'=2,'r1'=2,'g'=4,'r0'=2] {'r1','r0'}, dimensions={0} | all-to-all | bytes 98304 | tf_op jit(solution)/shard_map/all_to_all | solution.py:370
  50.8 0.1 last.1
  50.8 25.4 %all_to_all.33.arrived = f32[32,16,128]{2,1,0:T(8,128)S(1)} all-to-all(f32[32,16,128]{2,1,0:T(8,128)S(1)} %last.1), channel_id=1, replica_groups=mesh['freq'=16,'c'=2,'r1'=2,'g'=4,'r0'=2] {'freq','c'}, dimensions={0} | all-to-all | bytes 524288 | tf_op jit(solution)/shard_map/all_to_all | solution.py:370
  76.3 0.1 joined.1
  76.4 14.8 %all_to_all.34 = f32[16,64,128]{2,1,0:T(8,128)S(1)} all-to-all(f32[16,64,128]{2,1,0:T(8,128)S(1)} %joined.1), channel_id=1, replica_groups=mesh['freq'=16,'c'=2,'r1'=2,'g'=4,'r0'=2] {'r1','g','r0'}, dimensions={0} | all-to-all | bytes 1048576 | tf_op jit(solution)/shard_map/all_to_all | solution.py:370
  91.2 5.0 %collective-permute-start = (f32[16,32,128]{2,1,0:T(8,128)S(1)}, f32[16,32,128]{2,1,0:T(8,128)S(1)}, u32[]{:S(2)}, u32[]{:S(2)}) collective-permute-start(f32[16,32,128]{2,1,0:T(8,128)S(1)} %slice.4), channel_id=1, source_target_pairs={{0,32},{32,0},{64,96},{96,64},{128,160},{160,128},{192,224},{224,1... | collective-permute-start | bytes 786440 | tf_op jit(solution)/shard_map/ppermute | solution.py:446
  96.2 0.0 copy-done
  96.2 1.1 %near.1 = (f32[2,8,8,512]{3,2,1,0:T(8,128)}, f32[4,8,8,512]{3,2,1,0:T(8,128)}, f32[2,8,8,512]{3,2,1,0:T(8,128)S(1)}) custom-call(f32[1024,128]{1,0:T(8,128)S(1)} %bitcast.3, f32[2,8,8,512]{3,2,1,0:T(8,128)S(1)} %copy-done), custom_call_target="tpu_custom_call" | custom-call | flops 1000000 | bytes 2000000 | tf_op jit(solution)/shard_map/near/pallas_call | solution.py:451
  97.3 0.0 collective-permute-done
  97.3 1.0 far.1
  (1 shorter events, 0.0 us)
Async XLA Ops:
  2.5 22.0 %all-to-all-start = ((f32[8,32,128]{2,1,0:T(8,128)}), f32[8,32,128]{2,1,0:T(8,128)S(1)}, u32[]{:S(2)}, u32[]{:S(2)}) async-start(f32[8,32,128]{2,1,0:T(8,128)} %pack.1), calls=%async_computation | async-start | bytes 262144 | tf_op jit(solution)/shard_map/all_to_all | solution.py:370
  44.6 51.6 %copy-start = (f32[2,8,8,512]{3,2,1,0:T(8,128)S(1)}, f32[2,8,8,512]{3,2,1,0:T(8,128)}, u32[]{:S(2)}) copy-start(f32[2,8,8,512]{3,2,1,0:T(8,128)} %duals_ref.3) | copy-start | bytes 786436
  91.2 6.1 %collective-permute-start = (f32[16,32,128]{2,1,0:T(8,128)S(1)}, f32[16,32,128]{2,1,0:T(8,128)S(1)}, u32[]{:S(2)}, u32[]{:S(2)}) collective-permute-start(f32[16,32,128]{2,1,0:T(8,128)S(1)} %slice.4), channel_id=1, source_target_pairs={{0,32},{32,0},{64,96},{96,64},{128,160},{160,128},{192,224},{224,1... | collective-permute-start | bytes 786440 | tf_op jit(solution)/shard_map/ppermute | solution.py:446

commit v5 on v4

--- a/solution.py
+++ b/solution.py
@@ -21,6 +21,7 @@
 GROUPS = 4
 PAIR = DIRS // GROUPS
 SOURCES = CHANS * GROUPS
+HALF = 4
 F32 = jnp.float32
 BF16 = jnp.bfloat16
 
@@ -280,7 +281,7 @@
     summed(split(rest), rows_ref, at_ref, hot_ref, terms, out_ref)
 
 
-def last_kernel(damping, arrived, gains_ref, own_ref, out_ref, total_ref, new_ref):
+def last_kernel(damping, arrived, gains_ref, own_ref, out_ref, total_ref, mixed_ref):
     value = arrived[0]
     for n in range(1, arrived.shape[0]):
         value = value + arrived[n]
@@ -290,80 +291,67 @@
     duals, prior = [[own_ref[n, pl.ds(i, PAIR, stride=8), :] for i in range(8)] for n in (1, 2)]
     new = stepped(total, gains, duals, prior, damping)
     for i in range(8):
-        new_ref[pl.ds(i, PAIR, stride=8), :] = new[i]
-    mixed = new_ref[...] + own_ref[1] / RHO
+        mixed_ref[i // HALF, pl.ds(i % HALF, PAIR, stride=HALF), :] = new[i] + duals[i] / RHO
     for n in range(out_ref.shape[0]):
-        out_ref[n] = mixed
+        out_ref[n] = mixed_ref[n // CHANS % 2]
 
 
 def joined_kernel(weights, arrived, out_ref):
     freq = lax.axis_index("freq")
-    first = freq % 2 == 0
-    parts = [arrived[freq * CHANS + c] for c in range(CHANS)]
+    twin = freq + 1 - 2 * (freq % 2)
+    parts = [arrived[f * CHANS + c] for f in (freq, twin) for c in range(CHANS)]
     mixed = [arrived[n] for n in range(arrived.shape[0])]
-    for j in range(2):
-        total = None
-        for n, value in enumerate(mixed):
-            weight = jnp.where(first, float(weights[j, n]), float(weights[j + 2, n]))
-            total = weight * value if total is None else total + weight * value
+    for j in range(POLY):
+        total = float(weights[j, 0]) * mixed[0]
+        for n in range(1, len(mixed)):
+            total = total + float(weights[j, n]) * mixed[n]
         parts.append(total)
     for n in range(out_ref.shape[0]):
         for k, part in enumerate(parts):
-            out_ref[n, pl.ds(k * 16, 16), :] = part
+            out_ref[n, pl.ds(k * 8, 8), :] = part
 
 
 def tile_of(ref, q, row, size):
     place = (q // 2) * 8 + q % 2
     return jnp.concatenate(
-        [ref[pl.ds(place * size + row + d * 8, GROUPS, stride=2 * size), :] for d in range(PAIR)], axis=0
-    )
-
-
-def sides(count):
+        [ref[pl.ds(place * size + row + d * HALF, GROUPS, stride=2 * size), :] for d in range(PAIR)], axis=0
+    )
+
+
+def put_half(count, far, ref, size, poly_at, duals_ref, outs, held, sems):
     freq = lax.axis_index("freq")
-    core = freq % 2
+    side = 1 - freq % 2 if far else freq % 2
     basis = [basis_of(freq * CHANS + c, count) for c in range(CHANS)]
-    mine = [[jnp.where(core == 0, b[j], b[j + 2]) for j in range(2)] for b in basis]
-    his = [[jnp.where(core == 0, b[j + 2], b[j]) for j in range(2)] for b in basis]
-    return core, mine, his
-
-
-def near_kernel(count, all_ref, duals_ref, gains_out, poly_out, part_ref, gains, poly, sems):
-    core, mine, _ = sides(count)
-    to_gains = pltpu.make_async_copy(gains, gains_out, sems.at[0])
-    to_poly = pltpu.make_async_copy(poly, poly_out.at[pl.ds(2 * core, 2)], sems.at[1])
-    for i in range(8):
-        for q in range(CUTS):
-            lanes = slice(q * LANES, (q + 1) * LANES)
-            for j in range(2):
-                poly[j, i, :, lanes] = tile_of(all_ref, q, 32 + j * 16 + i, 64)
+    gains, duals, poly = held
+    to_gains, to_duals, to_poly = [
+        pltpu.make_async_copy(a, b.at[:, pl.ds(HALF * side, HALF)], sems.at[n])
+        for n, (a, b) in enumerate(zip(held, outs))
+    ]
+    for i in range(HALF):
+        for j in range(POLY):
+            for q in range(CUTS):
+                poly[j, i, :, q * LANES : (q + 1) * LANES] = tile_of(ref, q, poly_at + j * 8 + i, size)
     to_poly.start()
     for c in range(CHANS):
-        for i in range(8):
-            mixed = jnp.concatenate([tile_of(all_ref, q, c * 16 + i, 64) for q in range(CUTS)], axis=1)
-            gains[c, i] = mixed - duals_ref[c, i] / RHO
-            part_ref[c, i] = RHO * (mixed - (mine[c][0] * poly[0, i] + mine[c][1] * poly[1, i]))
+        for i in range(HALF):
+            mixed = jnp.concatenate([tile_of(ref, q, c * 8 + i, size) for q in range(CUTS)], axis=1)
+            gains[c, i] = mixed - duals_ref[c, HALF * side + i] / RHO
+            duals[c, i] = RHO * (mixed - sum(basis[c][j] * poly[j, i] for j in range(POLY)))
     to_gains.start()
+    to_duals.start()
     to_poly.wait()
     to_gains.wait()
-
-
-def far_kernel(count, other_ref, part_ref, half_ref, duals_out, poly_out, duals, poly, sems):
-    del half_ref
-    core, _, his = sides(count)
-    to_duals = pltpu.make_async_copy(duals, duals_out, sems.at[0])
-    to_poly = pltpu.make_async_copy(poly, poly_out.at[pl.ds(2 - 2 * core, 2)], sems.at[1])
-    for i in range(8):
-        for q in range(CUTS):
-            for j in range(2):
-                poly[j, i, :, q * LANES : (q + 1) * LANES] = tile_of(other_ref, q, j * 16 + i, 32)
-    to_poly.start()
-    for c in range(CHANS):
-        for i in range(8):
-            duals[c, i] = part_ref[c, i] - RHO * (his[c][0] * poly[0, i] + his[c][1] * poly[1, i])
-    to_duals.start()
-    to_poly.wait()
     to_duals.wait()
+
+
+def near_kernel(count, ref, duals_ref, gains_out, duals_out, poly_out, gains, duals, poly, sems):
+    outs = (gains_out, duals_out, poly_out)
+    put_half(count, False, ref, 64, 32, duals_ref, outs, (gains, duals, poly), sems)
+
+
+def far_kernel(count, ref, duals_ref, _g, _d, _p, gains_out, duals_out, poly_out, gains, duals, poly, sems):
+    outs = (gains_out, duals_out, poly_out)
+    put_half(count, True, ref, 48, 16, duals_ref, outs, (gains, duals, poly), sems)
 
 
 def exchanged(x, axis):
@@ -432,43 +420,42 @@
     sums = exchanged(sums, ("r1", "r0"))
     mixed = call(
         functools.partial(last_kernel, 6.0),
-        (freqs * CHANS, *share),
+        (freqs * CHANS, 8, LANES),
         sums,
         gains,
         cut,
-        scratch=[pltpu.VMEM((24, LANES), F32), pltpu.VMEM(share, F32)],
+        scratch=[pltpu.VMEM((24, LANES), F32), pltpu.VMEM((2, 8, LANES), F32)],
         name="last",
     )
     mixed = exchanged(mixed, ("freq", "c"))
     members = times // CHANS
     copies = call(functools.partial(joined_kernel, fit_weights(count)), (members, 64, LANES), mixed, name="joined")
     everything = exchanged(copies, ("r1", "g", "r0"))
-    other = lax.ppermute(everything[:, 32:], "freq", [(i, i ^ 1) for i in range(freqs)])
+    other = lax.ppermute(everything[:, 16:], "freq", [(i, i ^ 1) for i in range(freqs)])
     block = (CHANS, 8, DIRS, STATIONS)
-    held = [pltpu.VMEM(block, F32), pltpu.VMEM(block, F32), pltpu.SemaphoreType.DMA((2,))]
-    full = (POLY, 8, DIRS, STATIONS)
-    everything = in_vmem(everything.reshape(members * 64, LANES))
-    gains, half, part = pl.pallas_call(
+    outs = (pltpu.HBM(block, F32), pltpu.HBM(block, F32), pltpu.HBM((POLY, 8, DIRS, STATIONS), F32))
+    held = [pltpu.VMEM((n, HALF, DIRS, STATIONS), F32) for n in (CHANS, CHANS, POLY)]
+    options = dict(
+        out_shape=outs,
+        out_specs=(HBM, HBM, HBM),
+        scratch_shapes=[*held, pltpu.SemaphoreType.DMA((3,))],
+        compiler_params=pltpu.CompilerParams(vmem_limit_bytes=12 << 20),
+    )
+    duals_start = in_vmem(duals_start)
+    halves = pl.pallas_call(
         functools.partial(near_kernel, count),
-        out_shape=(pltpu.HBM(block, F32), pltpu.HBM(full, F32), pltpu.VMEM(block, F32)),
         in_specs=[VMEM, VMEM],
-        out_specs=(HBM, HBM, VMEM),
-        scratch_shapes=held,
-        compiler_params=pltpu.CompilerParams(vmem_limit_bytes=12 << 20),
         cost_estimate=pl.CostEstimate(flops=1000000, bytes_accessed=2000000, transcendentals=0),
         name="near",
-    )(everything, in_vmem(duals_start))
-    duals, polynomial = pl.pallas_call(
+        **options,
+    )(in_vmem(everything.reshape(members * 64, LANES)), duals_start)
+    return pl.pallas_call(
         functools.partial(far_kernel, count),
-        out_shape=(pltpu.HBM(block, F32), pltpu.HBM(full, F32)),
-        in_specs=[VMEM, VMEM, HBM],
-        out_specs=(HBM, HBM),
-        input_output_aliases={2: 1},
-        scratch_shapes=held,
-        compiler_params=pltpu.CompilerParams(vmem_limit_bytes=12 << 20),
+        in_specs=[VMEM, VMEM, HBM, HBM, HBM],
+        input_output_aliases={2: 0, 3: 1, 4: 2},
         name="far",
-    )(in_vmem(other.reshape(members * 32, LANES)), part, half)
-    return (gains, duals, polynomial)
+        **options,
+    )(in_vmem(other.reshape(members * 48, LANES)), duals_start, *halves)
 
 
 def solution(mesh):

time: 99.5 us -> 97.3 us (0.978)
  blocking collectives: 63.4 us -> 61.1 us
    all_to_all x5, blocking collectives: 63.4 us -> 61.1 us  [exchanged(): return lax.all_to_all(x, axis, split_axis=0, concat_axis=0, tiled=True)]
  transfers between devices with their start and end apart: 2 -> 2, of which waited for: 1 -> 2; matrix products, arithmetic and copies ran while one was open for 0% -> 0% of each run, Pallas kernels for 3% -> 3%
where the time goes in v5:
time: 97.3 us; the launch traced here: 96.3 us
  blocking collectives  61.1 us (63%)
  starting transfers between devices  17.9 us (18%)
  Pallas kernels  8.46 us (9%)
  waiting for transfers between devices  8.05 us (8%)
    all_to_all x5, blocking collectives, exchanged(): return lax.all_to_all(x, axis, split_axis=0, concat_axis=0, tiled=True)  61.1 us
    all_to_all x1, starting transfers between devices, exchanged(): return lax.all_to_all(x, axis, split_axis=0, concat_axis=0, tiled=True)  12.9 us
    all_to_all x1, waiting for transfers between devices, exchanged(): return lax.all_to_all(x, axis, split_axis=0, concat_axis=0, tiled=True)  7.73 us
    pallas_call x7, Pallas kernels, call(): pl.pallas_call(kernel, out_shape=tuple((pltpu.VMEM(o, t) for o, t in zip(...  6.47 us
    ppermute x1, starting transfers between devices, shards(): lax.ppermute(everything[:, 16:], 'freq', [(i, i ^ 1) for i in range(freqs)])  5.04 us
  transfers between devices with their start and end apart: 2, of which 2 were waited for; matrix products, arithmetic and copies ran while one was open for 0% of the time, Pallas kernels for 3%

profile of v5, /device:TPU:1, one launch (start us, length us, event | category | flops | bytes accessed | tf_op | source)
XLA Modules:
  0.0 96.3 jit_solution(17305623263806008985)
XLA Ops:
  0.6 1.9 %pack.1 = f32[8,32,128]{2,1,0:T(8,128)} custom-call(f32[2,8,8,512]{3,2,1,0:T(8,128)} %gains_ref.3, bf16[2,8,8,128]{3,2,1,0:T(8,128)(2,1)} %coh_ref.1, f32[2,8,128]{2,1,0:T(8,128)} %vis_ref.1, s32[2,128]{1,0:T(2,128)} %pairs_ref.1), custom_call_target="tpu_custom_call" | custom-call | tf_op jit(solution)/shard_map/pack/pallas_call | solution.py:75
  2.5 12.9 %all-to-all-start = ((f32[8,32,128]{2,1,0:T(8,128)}), f32[8,32,128]{2,1,0:T(8,128)S(1)}, u32[]{:S(2)}, u32[]{:S(2)}) async-start(f32[8,32,128]{2,1,0:T(8,128)} %pack.1), calls=%async_computation | async-start | bytes 262144 | tf_op jit(solution)/shard_map/all_to_all | solution.py:358
  15.4 1.4 %own.1 = (f32[3,64,128]{2,1,0:T(8,128)S(1)}, f32[3,16,128]{2,1,0:T(8,128)S(1)}) custom-call(f32[2,8,8,512]{3,2,1,0:T(8,128)} %gains_ref.3, f32[2,8,8,512]{3,2,1,0:T(8,128)} %duals_ref.5, f32[4,8,8,512]{3,2,1,0:T(8,128)} %poly_ref.1), custom_call_target="tpu_custom_call" | custom-call | tf_op jit(solution)/shard_map/own/pallas_call | solution.py:75
  16.8 7.7 %all-to-all-done = f32[8,32,128]{2,1,0:T(8,128)S(1)} async-done(((f32[8,32,128]{2,1,0:T(8,128)}), f32[8,32,128]{2,1,0:T(8,128)S(1)}, u32[]{:S(2)}, u32[]{:S(2)}) %all-to-all-start) | async-done | bytes 131104 | tf_op jit(solution)/shard_map/all_to_all | solution.py:358
  24.6 1.7 %start.1 = (f32[4,96,128]{2,1,0:T(8,128)S(1)}, bf16[512,2048]{1,0:T(8,128)(2,1)S(1)}, f32[64,128]{1,0:T(8,128)S(1)}) custom-call(f32[256,128]{1,0:T(8,128)S(1)} %bitcast.4, f32[3,64,128]{2,1,0:T(8,128)S(1)} %get-tuple-element.14.own_ref), custom_call_target="tpu_custom_call" | custom-call | tf_op jit(solution)/shard_map/start/pallas_call | solution.py:75
  26.3 7.4 %all_to_all.30.arrived = f32[4,96,128]{2,1,0:T(8,128)S(1)} all-to-all(f32[4,96,128]{2,1,0:T(8,128)S(1)} %get-tuple-element.15), channel_id=1, replica_groups=mesh['freq'=16,'c'=2,'r1'=2,'g'=4,'r0'=2] {'r1','r0'}, dimensions={0} | all-to-all | bytes 393216 | tf_op jit(solution)/shard_map/all_to_all | solution.py:358
  33.7 0.5 middle.1
  34.2 9.6 %all_to_all.31.arrived = f32[4,64,128]{2,1,0:T(8,128)S(1)} all-to-all(f32[4,64,128]{2,1,0:T(8,128)S(1)} %get-tuple-element.18), channel_id=1, replica_groups=mesh['freq'=16,'c'=2,'r1'=2,'g'=4,'r0'=2] {'g'}, dimensions={0} | all-to-all | bytes 262144 | tf_op jit(solution)/shard_map/all_to_all | solution.py:358
  43.8 0.8 second.1
  44.6 0.0 copy-start
  44.6 6.1 %all_to_all.32.arrived = f32[4,24,128]{2,1,0:T(8,128)S(1)} all-to-all(f32[4,24,128]{2,1,0:T(8,128)S(1)} %second.1), channel_id=1, replica_groups=mesh['freq'=16,'c'=2,'r1'=2,'g'=4,'r0'=2] {'r1','r0'}, dimensions={0} | all-to-all | bytes 98304 | tf_op jit(solution)/shard_map/all_to_all | solution.py:358
  50.8 23.2 %all_to_all.33.arrived = f32[32,8,128]{2,1,0:T(8,128)S(1)} all-to-all(f32[32,8,128]{2,1,0:T(8,128)S(1)} %last.1), channel_id=1, replica_groups=mesh['freq'=16,'c'=2,'r1'=2,'g'=4,'r0'=2] {'freq','c'}, dimensions={0} | all-to-all | bytes 262144 | tf_op jit(solution)/shard_map/all_to_all | solution.py:358
  74.0 0.1 joined.1
  74.1 14.8 %all_to_all.34 = f32[16,64,128]{2,1,0:T(8,128)S(1)} all-to-all(f32[16,64,128]{2,1,0:T(8,128)S(1)} %joined.1), channel_id=1, replica_groups=mesh['freq'=16,'c'=2,'r1'=2,'g'=4,'r0'=2] {'r1','g','r0'}, dimensions={0} | all-to-all | bytes 1048576 | tf_op jit(solution)/shard_map/all_to_all | solution.py:358
  88.9 5.0 %collective-permute-start = (f32[16,48,128]{2,1,0:T(8,128)S(1)}, f32[16,48,128]{2,1,0:T(8,128)S(1)}, u32[]{:S(2)}, u32[]{:S(2)}) collective-permute-start(f32[16,48,128]{2,1,0:T(8,128)S(1)} %slice.4), channel_id=1, source_target_pairs={{0,32},{32,0},{64,96},{96,64},{128,160},{160,128},{192,224},{224,1... | collective-permute-start | bytes 1179656 | tf_op jit(solution)/shard_map/ppermute | solution.py:434
  94.0 0.0 copy-done
  94.0 1.0 %near.1 = (f32[2,8,8,512]{3,2,1,0:T(8,128)}, f32[2,8,8,512]{3,2,1,0:T(8,128)}, f32[4,8,8,512]{3,2,1,0:T(8,128)}) custom-call(f32[1024,128]{1,0:T(8,128)S(1)} %bitcast.3, f32[2,8,8,512]{3,2,1,0:T(8,128)S(1)} %copy-done), custom_call_target="tpu_custom_call" | custom-call | flops 1000000 | bytes 2000000 | tf_op jit(solution)/shard_map/near/pallas_call | solution.py:445
  95.0 0.3 collective-permute-done
  95.3 1.0 %far.1 = (f32[2,8,8,512]{3,2,1,0:T(8,128)}, f32[2,8,8,512]{3,2,1,0:T(8,128)}, f32[4,8,8,512]{3,2,1,0:T(8,128)}) custom-call(f32[768,128]{1,0:T(8,128)S(1)} %bitcast.7, f32[2,8,8,512]{3,2,1,0:T(8,128)S(1)} %copy-done, f32[2,8,8,512]{3,2,1,0:T(8,128)} %get-tuple-element.22._g, ...), custom_call_target="tpu_custom_call", output_to_operand_aliasing={{0}: (2, {}), {1}: (3, {}), {2}: (4, {})} | custom-call | tf_op jit(solution)/shard_map/far/pallas_call | solution.py:452
  (2 shorter events, 0.1 us)
Async XLA Ops:
  2.5 22.0 %all-to-all-start = ((f32[8,32,128]{2,1,0:T(8,128)}), f32[8,32,128]{2,1,0:T(8,128)S(1)}, u32[]{:S(2)}, u32[]{:S(2)}) async-start(f32[8,32,128]{2,1,0:T(8,128)} %pack.1), calls=%async_computation | async-start | bytes 262144 | tf_op jit(solution)/shard_map/all_to_all | solution.py:358
  44.6 49.4 %copy-start = (f32[2,8,8,512]{3,2,1,0:T(8,128)S(1)}, f32[2,8,8,512]{3,2,1,0:T(8,128)}, u32[]{:S(2)}) copy-start(f32[2,8,8,512]{3,2,1,0:T(8,128)} %duals_ref.5) | copy-start | bytes 786436
  88.9 6.4 %collective-permute-start = (f32[16,48,128]{2,1,0:T(8,128)S(1)}, f32[16,48,128]{2,1,0:T(8,128)S(1)}, u32[]{:S(2)}, u32[]{:S(2)}) collective-permute-start(f32[16,48,128]{2,1,0:T(8,128)S(1)} %slice.4), channel_id=1, source_target_pairs={{0,32},{32,0},{64,96},{96,64},{128,160},{160,128},{192,224},{224,1... | collective-permute-start | bytes 1179656 | tf_op jit(solution)/shard_map/ppermute | solution.py:434

commit v6 on v5

--- a/solution.py
+++ b/solution.py
@@ -63,19 +63,23 @@
 HBM = pl.BlockSpec(memory_space=pltpu.HBM)
 
 
+def in_hbm(x):
+    return pltpu.with_memory_space_constraint(x, pltpu.MemorySpace.HBM)
+
+
 def in_vmem(x):
     return pltpu.with_memory_space_constraint(x, pltpu.MemorySpace.VMEM)
 
 
-def call(kernel, outs, *args, scratch=(), fast=None, kinds=None, limit=12 << 20, name=None):
+def call(kernel, outs, *args, scratch=(), fast=None, kinds=None, far=(), limit=12 << 20, name=None):
     fast = range(len(args)) if fast is None else fast
-    args = [in_vmem(a) if n in fast else a for n, a in enumerate(args)]
+    args = [in_vmem(a) if n in fast else in_hbm(a) if n in far else a for n, a in enumerate(args)]
     many = isinstance(outs, list)
     kinds = kinds or [F32] * len(outs)
     return pl.pallas_call(
         kernel,
         out_shape=tuple(pltpu.VMEM(o, t) for o, t in zip(outs, kinds)) if many else pltpu.VMEM(outs, F32),
-        in_specs=[VMEM for _ in args],
+        in_specs=[HBM if n in far else VMEM for n in range(len(args))],
         out_specs=tuple(VMEM for _ in outs) if many else VMEM,
         scratch_shapes=list(scratch),
         compiler_params=pltpu.CompilerParams(vmem_limit_bytes=limit),
@@ -102,7 +106,7 @@
     return matrix[0] + matrix[1]
 
 
-def pack_kernel(gains_ref, coh_ref, vis_ref, pairs_ref, out_ref, sky):
+def pack_kernel(gains_ref, coh_ref, vis_ref, pairs_ref, out_ref, own_ref, sky):
     station = lax.broadcasted_iota(jnp.int32, (STATIONS, ROWS), 0)
     hot = [jnp.where(station == pairs_ref[i : i + 1, :], 1.0, 0.0) for i in range(2)]
     hot = jnp.concatenate(hot, axis=1).astype(BF16)
@@ -127,6 +131,9 @@
                 out_ref[c * GROUPS + g, pl.ds(d * 8, 8), :] = sky[c, pl.ds(d * GROUPS + g, 8, stride=DIRS), :]
             out_ref[c * GROUPS + g, pl.ds(16, 8), :] = rest
             out_ref[c * GROUPS + g, pl.ds(24, 8), :] = names
+    _, c, g, _ = place_of()
+    for i in range(8):
+        to_rows(gains_ref[c, i], i, g, own_ref)
 
 
 def place_of():
@@ -134,26 +141,15 @@
     return lax.axis_index("freq"), lax.axis_index("c"), lax.axis_index("g"), own
 
 
-def own_kernel(count, gains_ref, duals_ref, poly_ref, out_ref, cut_ref):
-    freq, c, g, own = place_of()
-    basis = basis_of(freq * CHANS + c, count)
+def to_rows(tile, i, g, put):
     sublane = lax.broadcasted_iota(jnp.int32, (DIRS, STATIONS), 0)
-    for i in range(8):
-        prior = basis[0] * poly_ref[0, i]
-        for j in range(1, POLY):
-            prior += basis[j] * poly_ref[j, i]
-        for n, tile in enumerate((gains_ref[c, i], duals_ref[c, i], prior)):
-            for d in range(PAIR):
-                row = jnp.sum(jnp.where(sublane == d * GROUPS + g, tile, 0.0), axis=0, keepdims=True)
-                parts = [row[:, q * LANES : (q + 1) * LANES] for q in range(CUTS)]
-                chosen = parts[0]
-                for q in range(CUTS):
-                    out_ref[n, pl.ds(i * 8 + q * PAIR + d, 1), :] = parts[q]
-                    chosen = jnp.where(own == q, parts[q], chosen)
-                cut_ref[n, pl.ds(d * 8 + i, 1), :] = chosen
-
-
-def looked_up(gains_ref, hot_ref, at_ref):
+    for d in range(PAIR):
+        row = jnp.sum(jnp.where(sublane == d * GROUPS + g, tile, 0.0), axis=0, keepdims=True)
+        for q in range(CUTS):
+            put[pl.ds(i * 8 + q * PAIR + d, 1), :] = row[:, q * LANES : (q + 1) * LANES]
+
+
+def by_component(gains_ref):
     rows = jnp.concatenate(
         [
             jnp.concatenate(
@@ -163,10 +159,14 @@
         ],
         axis=0,
     )
-    found = jnp.dot(two_parts(rows), hot_ref[...], preferred_element_type=F32)
+    return two_parts(rows)
+
+
+def look_up(parts, hot, at_ref, block):
+    found = jnp.dot(parts, hot, preferred_element_type=F32)
     found = found[:16] + found[16:]
-    for b in range(2 * SOURCES):
-        at_ref[pl.ds(b * 16, 16), :] = found[:, b * ROWS : (b + 1) * ROWS]
+    for b in range(hot.shape[1] // ROWS):
+        at_ref[pl.ds((block + b) * 16, 16), :] = found[:, b * ROWS : (b + 1) * ROWS]
 
 
 def ends(at_ref, d):
@@ -209,14 +209,44 @@
     return model
 
 
-def start_kernel(rows_ref, own_ref, out_ref, hot_ref, model_ref, at, terms, total):
-    station = lax.broadcasted_iota(jnp.int32, (STATIONS, ROWS), 0).astype(F32)
-    for end in range(2):
-        for n in range(SOURCES):
-            name = rows_ref[pl.ds(n * 32 + 24 + end, 1), :]
-            lanes = pl.ds((end * SOURCES + n) * ROWS, ROWS)
-            hot_ref[:, lanes] = jnp.where(station == name, 1.0, 0.0).astype(BF16)
-    looked_up(own_ref.at[0], hot_ref, at)
+def start_kernel(
+    rows_ref,
+    own_ref,
+    duals_far,
+    poly_far,
+    out_ref,
+    hot_ref,
+    model_ref,
+    duals_ref,
+    poly_ref,
+    at,
+    terms,
+    total,
+    sems,
+):
+    loads = [
+        pltpu.make_async_copy(duals_far, duals_ref, sems.at[0]),
+        pltpu.make_async_copy(poly_far, poly_ref, sems.at[1]),
+    ]
+    for load in loads:
+        load.start()
+    shape = (STATIONS // 16, 16, ROWS)
+    station = lax.broadcasted_iota(jnp.int32, (STATIONS, ROWS), 0).astype(jnp.int16).reshape(shape)
+
+    def marked(name):
+        wide = jnp.broadcast_to(name.astype(jnp.int32), (16, ROWS)).astype(jnp.int16)
+        mark = jnp.where(station == wide[None], jnp.ones((), BF16), jnp.zeros((), BF16))
+        return mark.reshape(STATIONS, ROWS)
+
+    parts = by_component(own_ref)
+    for b in range(0, 2 * SOURCES, 2):
+        hot = []
+        for n in (b, b + 1):
+            end, source = n // SOURCES, n % SOURCES
+            hot.append(marked(rows_ref[pl.ds(source * 32 + 24 + end, 1), :]))
+        hot = jnp.concatenate(hot, axis=1)
+        hot_ref[:, b * ROWS : (b + 2) * ROWS] = hot
+        look_up(parts, hot, at, b)
     rest = split([rows_ref[pl.ds(16 + i, SOURCES, stride=32), :] for i in range(8)])
     summed(rest, rows_ref, at, hot_ref, terms, total)
     for q in range(CUTS):
@@ -227,6 +257,8 @@
     model = model_of(rows_ref, at)
     for i in range(8):
         model_ref[pl.ds(i * 8, 8), :] = model[i]
+    for load in loads:
+        load.wait()
 
 
 def stepped(total, gains, duals, prior, damping):
@@ -246,24 +278,42 @@
 
 
 def middle_kernel(
-    damping, arrived, own_ref, rows_ref, hot_ref, model_ref, out_ref, cut_ref, at_ref, gains_ref
+    damping,
+    count,
+    arrived,
+    own_ref,
+    duals_ref,
+    poly_ref,
+    rows_ref,
+    hot_ref,
+    model_ref,
+    out_ref,
+    cut_ref,
+    at_ref,
+    gains_ref,
+    other_ref,
 ):
-    own = place_of()[3]
+    freq, c, g, own = place_of()
+    basis = basis_of(freq * CHANS + c, count)
+    for i in range(8):
+        to_rows(duals_ref[c, i], i, g, other_ref.at[0])
+        to_rows(sum(basis[j] * poly_ref[j, i] for j in range(POLY)), i, g, other_ref.at[1])
     total = []
     for i in range(12):
         value = arrived[0, pl.ds(i * 8, 8), :]
         for n in range(1, arrived.shape[0]):
             value = value + arrived[n, pl.ds(i * 8, 8), :]
         total.append(value)
-    start = [[own_ref[n, pl.ds(i * 8, 8), :] for i in range(8)] for n in range(3)]
+    start = [[ref[pl.ds(i * 8, 8), :] for i in range(8)] for ref in (own_ref, other_ref.at[0], other_ref.at[1])]
     new = stepped(total, *start, damping)
     for i in range(8):
         gains_ref[pl.ds(i * 8, 8), :] = new[i]
-        chosen = new[i][:PAIR]
-        for q in range(1, CUTS):
-            chosen = jnp.where(own == q, new[i][q * PAIR : (q + 1) * PAIR], chosen)
-        cut_ref[pl.ds(i, PAIR, stride=8), :] = chosen
-    looked_up(gains_ref, hot_ref, at_ref)
+        for n, tile in enumerate((new[i], start[1][i], start[2][i])):
+            chosen = tile[:PAIR]
+            for q in range(1, CUTS):
+                chosen = jnp.where(own == q, tile[q * PAIR : (q + 1) * PAIR], chosen)
+            cut_ref[n, pl.ds(i, PAIR, stride=8), :] = chosen
+    look_up(by_component(gains_ref), hot_ref[...], at_ref, 0)
     model = model_of(rows_ref, at_ref)
     for i in range(8):
         change = model_ref[pl.ds(i * 8, 8), :] - model[i]
@@ -281,14 +331,13 @@
     summed(split(rest), rows_ref, at_ref, hot_ref, terms, out_ref)
 
 
-def last_kernel(damping, arrived, gains_ref, own_ref, out_ref, total_ref, mixed_ref):
+def last_kernel(damping, arrived, own_ref, out_ref, total_ref, mixed_ref):
     value = arrived[0]
     for n in range(1, arrived.shape[0]):
         value = value + arrived[n]
     total_ref[...] = value
     total = [total_ref[pl.ds(i, PAIR, stride=12), :] for i in range(12)]
-    gains = [gains_ref[pl.ds(i, PAIR, stride=8), :] for i in range(8)]
-    duals, prior = [[own_ref[n, pl.ds(i, PAIR, stride=8), :] for i in range(8)] for n in (1, 2)]
+    gains, duals, prior = [[own_ref[n, pl.ds(i, PAIR, stride=8), :] for i in range(8)] for n in range(3)]
     new = stepped(total, gains, duals, prior, damping)
     for i in range(8):
         mixed_ref[i // HALF, pl.ds(i % HALF, PAIR, stride=HALF), :] = new[i] + duals[i] / RHO
@@ -371,9 +420,9 @@
     work = pltpu.VMEM((2 * SOURCES * 24, ROWS), F32)
     quarters = (CUTS, 24, LANES)
 
-    sent = call(
+    sent, own = call(
         pack_kernel,
-        (SOURCES, 32, ROWS),
+        [(SOURCES, 32, ROWS), tiles],
         gains_start,
         coherencies,
         visibilities,
@@ -383,36 +432,39 @@
         scratch=[pltpu.VMEM((CHANS, 64, ROWS), F32)],
         name="pack",
     )
-    own, cut = call(
-        functools.partial(own_kernel, count),
-        [(3, *tiles), (3, *share)],
-        gains_start,
+    rows = exchanged(sent, ("c", "g")).reshape(SOURCES * 32, ROWS)
+    block = (CHANS, 8, DIRS, STATIONS)
+    full = (POLY, 8, DIRS, STATIONS)
+    sums, hot, model, duals_start, poly_start = call(
+        start_kernel,
+        [sums_shape, (STATIONS, 2 * SOURCES * ROWS), tiles, block, full],
+        rows,
+        own,
         duals_start,
         poly_start,
-        fast=[],
-        limit=60 << 20,
-        name="own",
-    )
-    rows = exchanged(sent, ("c", "g")).reshape(SOURCES * 32, ROWS)
-    sums, hot, model = call(
-        start_kernel,
-        [sums_shape, (STATIONS, 2 * SOURCES * ROWS), tiles],
-        rows,
-        own,
-        kinds=[F32, BF16, F32],
-        scratch=[pltpu.VMEM((2 * SOURCES * 16, ROWS), F32), work, pltpu.VMEM(quarters, F32)],
+        fast=[0, 1],
+        far=[2, 3],
+        kinds=[F32, BF16, F32, F32, F32],
+        scratch=[
+            pltpu.VMEM((2 * SOURCES * 16, ROWS), F32),
+            work,
+            pltpu.VMEM(quarters, F32),
+            pltpu.SemaphoreType.DMA((2,)),
+        ],
         name="start",
     )
     sums = exchanged(sums, ("r1", "r0"))
-    change, gains, at = call(
-        functools.partial(middle_kernel, 12.0),
-        [(GROUPS, *tiles), share, (2 * SOURCES * 16, ROWS)],
+    change, cut, at = call(
+        functools.partial(middle_kernel, 12.0, count),
+        [(GROUPS, *tiles), (3, *share), (2 * SOURCES * 16, ROWS)],
         sums,
         own,
+        duals_start,
+        poly_start,
         rows,
         hot,
         model,
-        scratch=[pltpu.VMEM(tiles, F32)],
+        scratch=[pltpu.VMEM(tiles, F32), pltpu.VMEM((2, *tiles), F32)],
         name="middle",
     )
     change = exchanged(change, "g")
@@ -422,7 +474,6 @@
         functools.partial(last_kernel, 6.0),
         (freqs * CHANS, 8, LANES),
         sums,
-        gains,
         cut,
         scratch=[pltpu.VMEM((24, LANES), F32), pltpu.VMEM((2, 8, LANES), F32)],
         name="last",
@@ -432,8 +483,7 @@
     copies = call(functools.partial(joined_kernel, fit_weights(count)), (members, 64, LANES), mixed, name="joined")
     everything = exchanged(copies, ("r1", "g", "r0"))
     other = lax.ppermute(everything[:, 16:], "freq", [(i, i ^ 1) for i in range(freqs)])
-    block = (CHANS, 8, DIRS, STATIONS)
-    outs = (pltpu.HBM(block, F32), pltpu.HBM(block, F32), pltpu.HBM((POLY, 8, DIRS, STATIONS), F32))
+    outs = (pltpu.HBM(block, F32), pltpu.HBM(block, F32), pltpu.HBM(full, F32))
     held = [pltpu.VMEM((n, HALF, DIRS, STATIONS), F32) for n in (CHANS, CHANS, POLY)]
     options = dict(
         out_shape=outs,

time: 97.3 us -> 96 us (0.987)
  blocking collectives: 61.1 us -> 82.8 us
  starting transfers between devices: 17.9 us -> 5.04 us
  waiting for transfers between devices: 8.05 us -> 0.32 us
  Pallas kernels: 8.46 us -> 6.14 us
    all_to_all x5 -> x6, blocking collectives: 61.1 us -> 82.8 us  [exchanged(): return lax.all_to_all(x, axis, split_axis=0, concat_axis=0, tiled=True)]
    all_to_all x1 -> x0, starting transfers between devices: 12.9 us -> none  [exchanged(): return lax.all_to_all(x, axis, split_axis=0, concat_axis=0, tiled=True)]
    all_to_all x1 -> x0, waiting for transfers between devices: 7.73 us -> none  [exchanged(): return lax.all_to_all(x, axis, split_axis=0, concat_axis=0, tiled=True)]
    pallas_call x7 -> x6, Pallas kernels: 6.47 us -> 4.15 us  [call(): pl.pallas_call(kernel, out_shape=tuple((pltpu.VMEM(o, t) for o, t in zip(...]
  transfers between devices with their start and end apart: 2 -> 1, of which waited for: 2 -> 1; matrix products, arithmetic and copies ran while one was open for 0% -> 0% of each run, Pallas kernels for 3% -> 1%
where the time goes in v6:
time: 96 us; the launch traced here: 95.1 us
  blocking collectives  82.8 us (86%)
  Pallas kernels  6.14 us (6%)
  starting transfers between devices  5.04 us (5%)
    all_to_all x6, blocking collectives, exchanged(): return lax.all_to_all(x, axis, split_axis=0, concat_axis=0, tiled=True)  82.8 us
    ppermute x1, starting transfers between devices, shards(): lax.ppermute(everything[:, 16:], 'freq', [(i, i ^ 1) for i in range(freqs)])  5.04 us
    pallas_call x6, Pallas kernels, call(): pl.pallas_call(kernel, out_shape=tuple((pltpu.VMEM(o, t) for o, t in zip(...  4.15 us
  transfers between devices with their start and end apart: 1, of which 1 were waited for; matrix products, arithmetic and copies ran while one was open for 0% of the time, Pallas kernels for 1%

profile of v6, /device:TPU:1, one launch (start us, length us, event | category | flops | bytes accessed | tf_op | source)
XLA Modules:
  0.0 95.1 jit_solution(1392582025829280122)
XLA Ops:
  0.6 1.3 %pack.1 = (f32[8,32,128]{2,1,0:T(8,128)S(1)}, f32[64,128]{1,0:T(8,128)S(1)}) custom-call(f32[2,8,8,512]{3,2,1,0:T(8,128)} %gains_ref.1, bf16[2,8,8,128]{3,2,1,0:T(8,128)(2,1)} %coh_ref.1, f32[2,8,128]{2,1,0:T(8,128)} %vis_ref.1, s32[2,128]{1,0:T(2,128)} %pairs_ref.1), custom_call_target="tpu_custom_call" | custom-call | tf_op jit(solution)/shard_map/pack/pallas_call | solution.py:79
  1.9 21.8 %all_to_all.30 = f32[8,32,128]{2,1,0:T(8,128)S(1)} all-to-all(f32[8,32,128]{2,1,0:T(8,128)S(1)} %get-tuple-element.16), channel_id=1, replica_groups=mesh['freq'=16,'c'=2,'r1'=2,'g'=4,'r0'=2] {'c','g'}, dimensions={0} | all-to-all | bytes 262144 | tf_op jit(solution)/shard_map/all_to_all | solution.py:407
  23.8 1.3 %start.1 = (f32[4,96,128]{2,1,0:T(8,128)S(1)}, bf16[512,2048]{1,0:T(8,128)(2,1)S(1)}, f32[64,128]{1,0:T(8,128)S(1)}, f32[2,8,8,512]{3,2,1,0:T(8,128)S(1)}, f32[4,8,8,512]{3,2,1,0:T(8,128)S(1)}) custom-call(f32[256,128]{1,0:T(8,128)S(1)} %bitcast.4, f32[64,128]{1,0:T(8,128)S(1)} %get-tuple-element.17.own_ref, f32[2,8,8,512]{3,2,1,0:T(8,128)} %duals_far.1, ...), custom_call_target="tpu_custom_call" | custom-call | tf_op jit(solution)/shard_map/start/pallas_call | solution.py:79
  25.1 7.4 %all_to_all.31.arrived = f32[4,96,128]{2,1,0:T(8,128)S(1)} all-to-all(f32[4,96,128]{2,1,0:T(8,128)S(1)} %get-tuple-element.18), channel_id=1, replica_groups=mesh['freq'=16,'c'=2,'r1'=2,'g'=4,'r0'=2] {'r1','r0'}, dimensions={0} | all-to-all | bytes 393216 | tf_op jit(solution)/shard_map/all_to_all | solution.py:407
  32.4 0.7 middle.1
  33.1 9.6 %all_to_all.32.arrived = f32[4,64,128]{2,1,0:T(8,128)S(1)} all-to-all(f32[4,64,128]{2,1,0:T(8,128)S(1)} %get-tuple-element.23), channel_id=1, replica_groups=mesh['freq'=16,'c'=2,'r1'=2,'g'=4,'r0'=2] {'g'}, dimensions={0} | all-to-all | bytes 262144 | tf_op jit(solution)/shard_map/all_to_all | solution.py:407
  42.7 0.8 second.1
  43.5 6.0 %all_to_all.33.arrived = f32[4,24,128]{2,1,0:T(8,128)S(1)} all-to-all(f32[4,24,128]{2,1,0:T(8,128)S(1)} %second.1), channel_id=1, replica_groups=mesh['freq'=16,'c'=2,'r1'=2,'g'=4,'r0'=2] {'r1','r0'}, dimensions={0} | all-to-all | bytes 98304 | tf_op jit(solution)/shard_map/all_to_all | solution.py:407
  49.6 23.2 %all_to_all.34.arrived = f32[32,8,128]{2,1,0:T(8,128)S(1)} all-to-all(f32[32,8,128]{2,1,0:T(8,128)S(1)} %last.1), channel_id=1, replica_groups=mesh['freq'=16,'c'=2,'r1'=2,'g'=4,'r0'=2] {'freq','c'}, dimensions={0} | all-to-all | bytes 262144 | tf_op jit(solution)/shard_map/all_to_all | solution.py:407
  72.8 0.1 joined.1
  72.9 14.8 %all_to_all.35 = f32[16,64,128]{2,1,0:T(8,128)S(1)} all-to-all(f32[16,64,128]{2,1,0:T(8,128)S(1)} %joined.1), channel_id=1, replica_groups=mesh['freq'=16,'c'=2,'r1'=2,'g'=4,'r0'=2] {'r1','g','r0'}, dimensions={0} | all-to-all | bytes 1048576 | tf_op jit(solution)/shard_map/all_to_all | solution.py:407
  87.7 5.0 %collective-permute-start = (f32[16,48,128]{2,1,0:T(8,128)S(1)}, f32[16,48,128]{2,1,0:T(8,128)S(1)}, u32[]{:S(2)}, u32[]{:S(2)}) collective-permute-start(f32[16,48,128]{2,1,0:T(8,128)S(1)} %slice.4), channel_id=1, source_target_pairs={{0,32},{32,0},{64,96},{96,64},{128,160},{160,128},{192,224},{224,1... | collective-permute-start | bytes 1179656 | tf_op jit(solution)/shard_map/ppermute | solution.py:485
  92.8 1.0 %near.1 = (f32[2,8,8,512]{3,2,1,0:T(8,128)}, f32[2,8,8,512]{3,2,1,0:T(8,128)}, f32[4,8,8,512]{3,2,1,0:T(8,128)}) custom-call(f32[1024,128]{1,0:T(8,128)S(1)} %bitcast.3, f32[2,8,8,512]{3,2,1,0:T(8,128)S(1)} %get-tuple-element.19.duals_ref), custom_call_target="tpu_custom_call" | custom-call | flops 1000000 | bytes 2000000 | tf_op jit(solution)/shard_map/near/pallas_call | solution.py:495
  93.8 0.3 collective-permute-done
  94.1 1.0 %far.1 = (f32[2,8,8,512]{3,2,1,0:T(8,128)}, f32[2,8,8,512]{3,2,1,0:T(8,128)}, f32[4,8,8,512]{3,2,1,0:T(8,128)}) custom-call(f32[768,128]{1,0:T(8,128)S(1)} %bitcast.7, f32[2,8,8,512]{3,2,1,0:T(8,128)S(1)} %get-tuple-element.19.duals_ref, f32[2,8,8,512]{3,2,1,0:T(8,128)} %get-tuple-element.26._g, ...), custom_call_target="tpu_custom_call", output_to_operand_aliasing={{0}: (2, {}), {1}: (3, {}), {2}: (4, {})} | custom-call | tf_op jit(solution)/shard_map/far/pallas_call | solution.py:502
  (2 shorter events, 0.1 us)
Async XLA Ops:
  87.7 6.4 %collective-permute-start = (f32[16,48,128]{2,1,0:T(8,128)S(1)}, f32[16,48,128]{2,1,0:T(8,128)S(1)}, u32[]{:S(2)}, u32[]{:S(2)}) collective-permute-start(f32[16,48,128]{2,1,0:T(8,128)S(1)} %slice.4), channel_id=1, source_target_pairs={{0,32},{32,0},{64,96},{96,64},{128,160},{160,128},{192,224},{224,1... | collective-permute-start | bytes 1179656 | tf_op jit(solution)/shard_map/ppermute | solution.py:485

commit v7 on v6

--- a/solution.py
+++ b/solution.py
@@ -372,9 +372,11 @@
     side = 1 - freq % 2 if far else freq % 2
     basis = [basis_of(freq * CHANS + c, count) for c in range(CHANS)]
     gains, duals, poly = held
-    to_gains, to_duals, to_poly = [
-        pltpu.make_async_copy(a, b.at[:, pl.ds(HALF * side, HALF)], sems.at[n])
-        for n, (a, b) in enumerate(zip(held, outs))
+    comps = pl.ds(HALF * side, HALF)
+    to_poly = pltpu.make_async_copy(poly, outs[2].at[:, comps], sems.at[0])
+    to_rest = [
+        [pltpu.make_async_copy(held[n].at[c], outs[n].at[c, comps], sems.at[1 + 2 * c + n]) for n in range(2)]
+        for c in range(CHANS)
     ]
     for i in range(HALF):
         for j in range(POLY):
@@ -386,11 +388,12 @@
             mixed = jnp.concatenate([tile_of(ref, q, c * 8 + i, size) for q in range(CUTS)], axis=1)
             gains[c, i] = mixed - duals_ref[c, HALF * side + i] / RHO
             duals[c, i] = RHO * (mixed - sum(basis[c][j] * poly[j, i] for j in range(POLY)))
-    to_gains.start()
-    to_duals.start()
+        for copy in to_rest[c]:
+            copy.start()
     to_poly.wait()
-    to_gains.wait()
-    to_duals.wait()
+    for copies in to_rest:
+        for copy in copies:
+            copy.wait()
 
 
 def near_kernel(count, ref, duals_ref, gains_out, duals_out, poly_out, gains, duals, poly, sems):
@@ -488,7 +491,7 @@
     options = dict(
         out_shape=outs,
         out_specs=(HBM, HBM, HBM),
-        scratch_shapes=[*held, pltpu.SemaphoreType.DMA((3,))],
+        scratch_shapes=[*held, pltpu.SemaphoreType.DMA((5,))],
         compiler_params=pltpu.CompilerParams(vmem_limit_bytes=12 << 20),
     )
     duals_start = in_vmem(duals_start)

time: 96 us -> 96 us (level)
  no operation moved by 1% of the time
where the time goes in v7:
time: 96 us; the launch traced here: 95.1 us
  blocking collectives  82.8 us (86%)
  Pallas kernels  6.14 us (6%)
  starting transfers between devices  5.04 us (5%)
    all_to_all x6, blocking collectives, exchanged(): return lax.all_to_all(x, axis, split_axis=0, concat_axis=0, tiled=True)  82.8 us
    ppermute x1, starting transfers between devices, shards(): lax.ppermute(everything[:, 16:], 'freq', [(i, i ^ 1) for i in range(freqs)])  5.04 us
    pallas_call x6, Pallas kernels, call(): pl.pallas_call(kernel, out_shape=tuple((pltpu.VMEM(o, t) for o, t in zip(...  4.15 us
  transfers between devices with their start and end apart: 1, of which 1 were waited for; matrix products, arithmetic and copies ran while one was open for 0% of the time, Pallas kernels for 1%

profile of v7, /device:TPU:1, one launch (start us, length us, event | category | flops | bytes accessed | tf_op | source)
XLA Modules:
  0.0 95.1 jit_solution(2904143497933565868)
XLA Ops:
  0.6 1.3 %pack.1 = (f32[8,32,128]{2,1,0:T(8,128)S(1)}, f32[64,128]{1,0:T(8,128)S(1)}) custom-call(f32[2,8,8,512]{3,2,1,0:T(8,128)} %gains_ref.1, bf16[2,8,8,128]{3,2,1,0:T(8,128)(2,1)} %coh_ref.1, f32[2,8,128]{2,1,0:T(8,128)} %vis_ref.1, s32[2,128]{1,0:T(2,128)} %pairs_ref.1), custom_call_target="tpu_custom_call" | custom-call | tf_op jit(solution)/shard_map/pack/pallas_call | solution.py:79
  1.9 21.8 %all_to_all.30 = f32[8,32,128]{2,1,0:T(8,128)S(1)} all-to-all(f32[8,32,128]{2,1,0:T(8,128)S(1)} %get-tuple-element.16), channel_id=1, replica_groups=mesh['freq'=16,'c'=2,'r1'=2,'g'=4,'r0'=2] {'c','g'}, dimensions={0} | all-to-all | bytes 262144 | tf_op jit(solution)/shard_map/all_to_all | solution.py:410
  23.8 1.3 %start.1 = (f32[4,96,128]{2,1,0:T(8,128)S(1)}, bf16[512,2048]{1,0:T(8,128)(2,1)S(1)}, f32[64,128]{1,0:T(8,128)S(1)}, f32[2,8,8,512]{3,2,1,0:T(8,128)S(1)}, f32[4,8,8,512]{3,2,1,0:T(8,128)S(1)}) custom-call(f32[256,128]{1,0:T(8,128)S(1)} %bitcast.4, f32[64,128]{1,0:T(8,128)S(1)} %get-tuple-element.17.own_ref, f32[2,8,8,512]{3,2,1,0:T(8,128)} %duals_far.1, ...), custom_call_target="tpu_custom_call" | custom-call | tf_op jit(solution)/shard_map/start/pallas_call | solution.py:79
  25.1 7.4 %all_to_all.31.arrived = f32[4,96,128]{2,1,0:T(8,128)S(1)} all-to-all(f32[4,96,128]{2,1,0:T(8,128)S(1)} %get-tuple-element.18), channel_id=1, replica_groups=mesh['freq'=16,'c'=2,'r1'=2,'g'=4,'r0'=2] {'r1','r0'}, dimensions={0} | all-to-all | bytes 393216 | tf_op jit(solution)/shard_map/all_to_all | solution.py:410
  32.4 0.7 middle.1
  33.1 9.6 %all_to_all.32.arrived = f32[4,64,128]{2,1,0:T(8,128)S(1)} all-to-all(f32[4,64,128]{2,1,0:T(8,128)S(1)} %get-tuple-element.23), channel_id=1, replica_groups=mesh['freq'=16,'c'=2,'r1'=2,'g'=4,'r0'=2] {'g'}, dimensions={0} | all-to-all | bytes 262144 | tf_op jit(solution)/shard_map/all_to_all | solution.py:410
  42.7 0.8 second.1
  43.5 6.0 %all_to_all.33.arrived = f32[4,24,128]{2,1,0:T(8,128)S(1)} all-to-all(f32[4,24,128]{2,1,0:T(8,128)S(1)} %second.1), channel_id=1, replica_groups=mesh['freq'=16,'c'=2,'r1'=2,'g'=4,'r0'=2] {'r1','r0'}, dimensions={0} | all-to-all | bytes 98304 | tf_op jit(solution)/shard_map/all_to_all | solution.py:410
  49.6 23.2 %all_to_all.34.arrived = f32[32,8,128]{2,1,0:T(8,128)S(1)} all-to-all(f32[32,8,128]{2,1,0:T(8,128)S(1)} %last.1), channel_id=1, replica_groups=mesh['freq'=16,'c'=2,'r1'=2,'g'=4,'r0'=2] {'freq','c'}, dimensions={0} | all-to-all | bytes 262144 | tf_op jit(solution)/shard_map/all_to_all | solution.py:410
  72.8 0.1 joined.1
  72.9 14.8 %all_to_all.35 = f32[16,64,128]{2,1,0:T(8,128)S(1)} all-to-all(f32[16,64,128]{2,1,0:T(8,128)S(1)} %joined.1), channel_id=1, replica_groups=mesh['freq'=16,'c'=2,'r1'=2,'g'=4,'r0'=2] {'r1','g','r0'}, dimensions={0} | all-to-all | bytes 1048576 | tf_op jit(solution)/shard_map/all_to_all | solution.py:410
  87.7 5.0 %collective-permute-start = (f32[16,48,128]{2,1,0:T(8,128)S(1)}, f32[16,48,128]{2,1,0:T(8,128)S(1)}, u32[]{:S(2)}, u32[]{:S(2)}) collective-permute-start(f32[16,48,128]{2,1,0:T(8,128)S(1)} %slice.4), channel_id=1, source_target_pairs={{0,32},{32,0},{64,96},{96,64},{128,160},{160,128},{192,224},{224,1... | collective-permute-start | bytes 1179656 | tf_op jit(solution)/shard_map/ppermute | solution.py:488
  92.8 1.0 %near.1 = (f32[2,8,8,512]{3,2,1,0:T(8,128)}, f32[2,8,8,512]{3,2,1,0:T(8,128)}, f32[4,8,8,512]{3,2,1,0:T(8,128)}) custom-call(f32[1024,128]{1,0:T(8,128)S(1)} %bitcast.3, f32[2,8,8,512]{3,2,1,0:T(8,128)S(1)} %get-tuple-element.19.duals_ref), custom_call_target="tpu_custom_call" | custom-call | flops 1000000 | bytes 2000000 | tf_op jit(solution)/shard_map/near/pallas_call | solution.py:498
  93.8 0.3 collective-permute-done
  94.1 1.0 %far.1 = (f32[2,8,8,512]{3,2,1,0:T(8,128)}, f32[2,8,8,512]{3,2,1,0:T(8,128)}, f32[4,8,8,512]{3,2,1,0:T(8,128)}) custom-call(f32[768,128]{1,0:T(8,128)S(1)} %bitcast.7, f32[2,8,8,512]{3,2,1,0:T(8,128)S(1)} %get-tuple-element.19.duals_ref, f32[2,8,8,512]{3,2,1,0:T(8,128)} %get-tuple-element.26._g, ...), custom_call_target="tpu_custom_call", output_to_operand_aliasing={{0}: (2, {}), {1}: (3, {}), {2}: (4, {})} | custom-call | tf_op jit(solution)/shard_map/far/pallas_call | solution.py:505
  (2 shorter events, 0.1 us)
Async XLA Ops:
  87.7 6.4 %collective-permute-start = (f32[16,48,128]{2,1,0:T(8,128)S(1)}, f32[16,48,128]{2,1,0:T(8,128)S(1)}, u32[]{:S(2)}, u32[]{:S(2)}) collective-permute-start(f32[16,48,128]{2,1,0:T(8,128)S(1)} %slice.4), channel_id=1, source_target_pairs={{0,32},{32,0},{64,96},{96,64},{128,160},{160,128},{192,224},{224,1... | collective-permute-start | bytes 1179656 | tf_op jit(solution)/shard_map/ppermute | solution.py:488
